TPU v7x, 128 devices: a whole 4x4x4 slice. The times are simulated.
128 devices in a mesh: stream: 64 (over z, y, x), seq: 2 (over core).
Axes of the slice: x: 4, y: 4, z: 4, core: 2. Of those that a mesh axis runs over, the one named last changes fastest.
Arguments:
- head_inputs: bfloat16 [64, 3072, 1536], P('stream', 'seq'), may hold values from -6 to 6
- state_maps: bfloat16 [64, 3072, 256], P('stream', 'seq'), may hold values from -2.1 to 2.1
- step_logits: float32 [64, 24, 3072], P('stream', None, 'seq'), may hold values from -3 to 5.5
- log_rates: float32 [24], replicated, may hold values from -7 to 0
- step_bias: float32 [24], replicated, may hold values from -6 to -2
- skip_gain: float32 [24], replicated, may hold values from 0.25 to 1.75
- old_states: float32 [64, 24, 64, 128], P('stream', 'seq'), may hold values from -6 to 6
- old_owner: int32 [64], replicated, may hold values from 0 to 63, as said below
- doc_starts: int32 [64, 2], P('stream'), may hold values from 0 to 3071
- grad_output: bfloat16 [64, 3072, 1536], P('stream', 'seq'), may hold values from -6 to 6
Outputs:
- layer_out: bfloat16 [64, 3072, 1536], P('stream', 'seq')
- grad_inputs: bfloat16 [64, 3072, 1536], P('stream', 'seq')
- grad_maps: bfloat16 [64, 3072, 256], P('stream', 'seq')
- grad_logits: float32 [64, 24, 3072], P('stream', None, 'seq')
- grad_rates: float32 [24], replicated
- grad_bias: float32 [24], replicated
- grad_skip: float32 [24], replicated
Inputs may be any that keep to these rules, and one draw needn't show every extreme that they name: A permutation of the 64 stream indices: new stream s continues old stream old_owner[s]. `doc_starts`: positions in a stream's segment where a document starts and the state is cleared; entries may repeat.
All inputs are finite; a program needn't handle non-finite values.
Results may differ from a plain program's by a relative error of at most 0.013.
Values sent between devices are 32-bit elements; how exact they have to be, the bound alone decides.
No kernel may reach another device: no remote copies, remote signals or barrier semaphores. Data moves between devices by JAX's collectives and lax.ppermute only.
A program may use at most 192 MiB of HBM per device.

v0:
```python
import jax
import jax.numpy as jnp
from jax import lax
from jax.sharding import PartitionSpec as P

GROUP = 256


def shifted_2(shard, axis, by):
    size = lax.axis_size(axis)
    pairs = [(i, i + by) for i in range(size) if 0 <= i + by < size]
    return lax.ppermute(shard, axis, pairs)


def decay_terms(logits_part, flags_part, log_rates, step_bias):
    step_size = jax.nn.softplus(logits_part + step_bias[:, None])
    cum_decay = jnp.cumsum(-step_size * jnp.exp(log_rates)[:, None], axis=-1)
    doc_index = jnp.cumsum(flags_part, axis=-1)
    return (step_size, cum_decay, doc_index)


def group_states(inputs_c, maps_c, logits_c, flags_c, log_rates, step_bias):
    step_size, cum_decay, doc_index = decay_terms(logits_c, flags_c, log_rates, step_bias)
    state_n = maps_c.shape[-1] // 2
    b_part = maps_c[:, :, :state_n].astype(jnp.float32)
    same_doc = doc_index == doc_index[:, -1:]
    weight = (
        jnp.where(same_doc[:, None, :], jnp.exp(cum_decay[:, :, -1:] - cum_decay), 0.0) * step_size
    )
    b_weighted = (weight[:, :, :, None] * b_part[:, None, :, :]).astype(jnp.bfloat16)
    states = jnp.einsum("cjhp,chjn->chpn", inputs_c, b_weighted, preferred_element_type=jnp.float32)
    decays = jnp.where(doc_index[:, -1:] == 0, jnp.exp(cum_decay[:, :, -1]), 0.0)
    return (states, decays)


def group_inputs(start_state, states, decays):

    def advance(carry, members):
        group_state, group_decay = members
        return (group_decay[:, None, None] * carry + group_state, carry)

    return lax.scan(advance, start_state, (states, decays))


def one_group(inputs_q, maps_q, logits_q, flags_q, starts_q, log_rates, step_bias, skip_gain):
    step_size, cum_decay, doc_index = decay_terms(logits_q, flags_q, log_rates, step_bias)
    state_n = maps_q.shape[-1] // 2
    b_part = maps_q[:, :state_n]
    c_part = maps_q[:, state_n:]
    scores = jnp.dot(c_part, b_part.T, preferred_element_type=jnp.float32)
    position = jnp.arange(maps_q.shape[0])
    visible = (position[None, :] <= position[:, None]) & (doc_index[None, :] == doc_index[:, None])
    log_gaps = jnp.where(visible[None], cum_decay[:, :, None] - cum_decay[:, None, :], -jnp.inf)
    mixing = (scores[None] * jnp.exp(log_gaps) * step_size[:, None, :]).astype(jnp.bfloat16)
    local_part = jnp.einsum("hij,jhp->ihp", mixing, inputs_q, preferred_element_type=jnp.float32)
    inflow = jnp.where(doc_index[None, :] == 0, jnp.exp(cum_decay), 0.0)
    carried = jnp.einsum(
        "in,hpn->ihp", c_part.astype(jnp.float32), starts_q, precision=lax.Precision.HIGHEST
    )
    summed = (
        local_part
        + carried * inflow.T[:, :, None]
        + skip_gain[None, :, None] * inputs_q.astype(jnp.float32)
    )
    return summed.reshape(inputs_q.shape[0], -1).astype(jnp.bfloat16)


def outputs(inputs_c, maps_c, logits_c, flags_c, log_rates, step_bias, skip_gain, starts_c):

    def per_group(carry, members):
        inputs_q, maps_q, logits_q, flags_q, starts_q = members
        return (
            carry,
            jax.checkpoint(one_group)(
                inputs_q, maps_q, logits_q, flags_q, starts_q, log_rates, step_bias, skip_gain
            ),
        )

    _, result = lax.scan(per_group, 0, (inputs_c, maps_c, logits_c, flags_c, starts_c))
    return result


def shards(
    head_inputs,
    state_maps,
    step_logits,
    log_rates,
    step_bias,
    skip_gain,
    old_states,
    old_owner,
    doc_starts,
    grad_output,
):
    length = head_inputs.shape[1]
    head_count = step_logits.shape[1]
    head_dim = old_states.shape[2]
    state_n = old_states.shape[3]
    groups = length // GROUP
    seq_index = lax.axis_index("seq")
    stream_index = lax.axis_index("stream")
    position = seq_index * length + lax.iota(jnp.int32, length)
    reset_flags = jnp.any(doc_starts[0][:, None] == position[None, :], axis=0).astype(jnp.int32)
    gathered = lax.all_gather(old_states, "stream", axis=0, tiled=True)
    own_block = lax.dynamic_index_in_dim(gathered, old_owner[stream_index], 0, keepdims=False)
    start_state = lax.all_gather(own_block, "seq", axis=0, tiled=True)
    inputs_c = head_inputs[0].reshape(groups, GROUP, head_count, head_dim)
    maps_c = state_maps[0].reshape(groups, GROUP, 2 * state_n)
    logits_c = step_logits[0].reshape(head_count, groups, GROUP).transpose(1, 0, 2)
    flags_c = reset_flags.reshape(groups, GROUP)

    def state_part(inputs_c, maps_c, logits_c, log_rates, step_bias):
        return group_states(inputs_c, maps_c, logits_c, flags_c, log_rates, step_bias)

    (states, decays), pull_states = jax.vjp(
        state_part, inputs_c, maps_c, logits_c, log_rates, step_bias
    )
    empty_state = jnp.zeros((head_count, head_dim, state_n), jnp.float32)
    local_state, _ = group_inputs(empty_state, states, decays)
    shard_decay = jnp.prod(decays, axis=0)
    is_first = seq_index == 0

    def forward_turn(counter, entering):
        leaving = shard_decay[:, None, None] * entering + local_state
        shifted = shifted_2(leaving, "seq", 1)
        return jnp.where(is_first, start_state, shifted)

    entry_state = lax.fori_loop(0, lax.axis_size("seq") - 1, forward_turn, start_state)
    (exit_state, starts_c), pull_inputs = jax.vjp(group_inputs, entry_state, states, decays)

    def output_part(inputs_c, maps_c, logits_c, log_rates, step_bias, skip_gain, starts_c):
        return outputs(
            inputs_c, maps_c, logits_c, flags_c, log_rates, step_bias, skip_gain, starts_c
        )

    result, pull_output = jax.vjp(
        output_part, inputs_c, maps_c, logits_c, log_rates, step_bias, skip_gain, starts_c
    )
    grads_c = grad_output[0].reshape(groups, GROUP, head_count * head_dim)
    in_first, maps_first, logits_first, rates_first, bias_first, skip_total, grad_starts = (
        pull_output(grads_c)
    )
    from_output = pull_inputs((jnp.zeros_like(exit_state), grad_starts))[0]

    def backward_turn(counter, leaving_grad):
        entering_grad = shard_decay[:, None, None] * leaving_grad + from_output
        return shifted_2(entering_grad, "seq", -1)

    exit_grad = lax.fori_loop(0, lax.axis_size("seq") - 1, backward_turn, empty_state)
    _, grad_states, grad_decays = pull_inputs((exit_grad, grad_starts))
    in_second, maps_second, logits_second, rates_second, bias_second = pull_states(
        (grad_states, grad_decays)
    )
    rates_total, bias_total, skip_sum = lax.psum(
        (rates_first + rates_second, bias_first + bias_second, skip_total), ("stream", "seq")
    )
    grad_logits = (logits_first + logits_second).transpose(1, 0, 2).reshape(1, head_count, length)
    return (
        result.reshape(1, length, -1),
        (in_first + in_second).reshape(1, length, -1),
        (maps_first + maps_second).reshape(1, length, -1),
        grad_logits,
        rates_total,
        bias_total,
        skip_sum,
    )


def solution(mesh):
    return jax.shard_map(
        shards,
        mesh=mesh,
        in_specs=(
            P("stream", "seq", None),
            P("stream", "seq", None),
            P("stream", None, "seq"),
            P(),
            P(),
            P(),
            P("stream", "seq", None, None),
            P(),
            P("stream", None),
            P("stream", "seq", None),
        ),
        out_specs=(
            P("stream", "seq", None),
            P("stream", "seq", None),
            P("stream", "seq", None),
            P("stream", None, "seq"),
            P(),
            P(),
            P(),
        ),
        check_vma=False,
    )
```

profile of v0, /device:TPU:0, one launch (start us, length us, event | category | flops | bytes accessed | tf_op | source)
XLA Modules:
  0.0 600.6 jit_solution(6530939128043399756)
XLA Ops:
  21.2 12.9 %reshape.634 = bf16[6,256,24,64]{3,2,1,0:T(8,128)(2,1)} reshape(bf16[1,1536,1536]{2,1,0:T(8,128)(2,1)} %param.22) | data formatting | bytes 9437184 | tf_op jit(solution)/shard_map/reshape;squeeze | solution.py:107
  34.1 10.3 %copy.231 = bf16[6,256,24,64]{1,3,2,0:T(8,128)(2,1)} copy(bf16[6,256,24,64]{3,2,1,0:T(8,128)(2,1)} %reshape.634) | data formatting | bytes 9437184
  46.2 8.0 %fusion.94 = f32[6,24,64,128]{3,2,1,0:T(8,128)} fusion(bf16[6,256,24,64]{1,3,2,0:T(8,128)(2,1)} %copy.231, f32[6,256,128]{1,2,0:T(8,128)S(1)} %copy.228, f32[6,24,256]{2,1,0:T(8,128)S(1)} %select_multiply_fusion.3), kind=kOutput, calls=%fused_computation.172 | convolution fusion | flops 613416960 | bytes 10371072 | tf_op jit(solution)/shard_map/jvp(cjhp,chjn->chpn)/dot_general | solution.py:31
  54.2 8.0 %while.108 = (s32[]{:T(128)}, f32[24,64,128]{2,1,0:T(8,128)S(1)}, f32[6,24]{1,0:T(8,128)S(1)}, f32[6,24,64,128]{3,2,1,0:T(8,128)}, s32[]{:T(128)}, /*index=5*/s32[]{:T(128)}) while((s32[]{:T(128)}, f32[24,64,128]{2,1,0:T(8,128)S(1)}, f32[6,24]{1,0:T(8,128)S(1)}, f32[6,24,64,128]{3,2,1,0:T(8,128)}, s32[]{:T(128)}, ...), condition=%wide.region_7.8_spmd.clone, body=%wide.region_6.7_spmd.clone.sunk | while | flops 589827 | bytes 2359671 | solution.py:42
  62.3 82.6 %all-gather.3.cloned.1.call-done = f32[64,12,64,128]{3,2,1,0:T(8,128)} async-done(((f32[1,12,64,128]{3,2,1,0:T(8,128)}), f32[64,12,64,128]{3,2,1,0:T(8,128)}) %all-gather.3.cloned.1.call-update) | async-done | bytes 25165840 | tf_op jit(solution)/shard_map/all_gather | solution.py:104
  156.4 17.0 %while.105 = (s32[]{:T(128)}, f32[24,64,128]{2,1,0:T(8,128)S(1)}, f32[6,24,64,128]{3,2,1,0:T(8,128)}, f32[6,24,1,1]{1,3,2,0:T(1,128)}, f32[6,24]{1,0:T(8,128)S(1)}, /*index=5*/f32[6,24,64,128]{3,2,1,0:T(8,128)}, s32[]{:T(128)}) while((s32[]{:T(128)}, f32[24,64,128]{2,1,0:T(8,128)S(1)}, f32[6,24,64,128]{3,2,1,0:T(8,128)}, ...), condition=%wide.region_9.10_spmd, body=%wide.region_8.9_spmd.sunk | while | flops 393218 | bytes 3934165 | solution.py:42
  180.5 195.7 %while.109 = (s32[]{:T(128)}, f32[24]{0:T(128)}, f32[24]{0:T(128)}, f32[24]{0:T(128)}, bf16[6,256,24,64]{1,3,2,0:T(8,128)(2,1)}, /*index=5*/bf16[6,256,256]{1,2,...) while((s32[]{:T(128)}, f32[24]{0:T(128)}, f32[24]{0:T(128)}, ...), condition=%wide.region_31.32_spmd.clone, body=%wide.region_16.31_spmd.clone.sunk | while | flops 2306163200 | bytes 22004424 | solution.py:79
  191.9 6.2 %fusion.183 = (f32[24,256]{1,0:T(8,128)S(1)}, f32[24,256]{1,0:T(8,128)S(1)}, f32[24,256]{1,0:T(8,128)}, bf16[256,256]{1,0:T(8,128)(2,1)S(1)}) fusion(f32[24,256]{1,0:T(8,128)S(1)} %copy_bitcast_fusion.13, f32[24,256]{1,0:T(8,128)} %get-tuple-element.1559, f32[256,256]{1,0:T(8,128)S(1)} %fusion.181, pred[256,256]{1,0:T(8,128)(4,1)S(1)} %fusion.182, ...), kind=kOutput, calls=%fused_computation.73.clone.1 | convolution fusion | flops 224835584 | bytes 2154496 | tf_op jit(solution)/shard_map/transpose(jvp())/while/body/eval_jaxpr/checkpoint/hij,jhp->ihp/dot_general | solution.py:55
  203.9 3.9 fusion.189
  224.5 6.2 %fusion.183 = (f32[24,256]{1,0:T(8,128)S(1)}, f32[24,256]{1,0:T(8,128)S(1)}, f32[24,256]{1,0:T(8,128)}, bf16[256,256]{1,0:T(8,128)(2,1)S(1)}) fusion(f32[24,256]{1,0:T(8,128)S(1)} %copy_bitcast_fusion.13, f32[24,256]{1,0:T(8,128)} %get-tuple-element.1559, f32[256,256]{1,0:T(8,128)S(1)} %fusion.181, pred[256,256]{1,0:T(8,128)(4,1)S(1)} %fusion.182, ...), kind=kOutput, calls=%fused_computation.73.clone.1 | convolution fusion | flops 224835584 | bytes 2154496 | tf_op jit(solution)/shard_map/transpose(jvp())/while/body/eval_jaxpr/checkpoint/hij,jhp->ihp/dot_general | solution.py:55
  236.5 3.9 fusion.189
  257.1 6.2 %fusion.183 = (f32[24,256]{1,0:T(8,128)S(1)}, f32[24,256]{1,0:T(8,128)S(1)}, f32[24,256]{1,0:T(8,128)}, bf16[256,256]{1,0:T(8,128)(2,1)S(1)}) fusion(f32[24,256]{1,0:T(8,128)S(1)} %copy_bitcast_fusion.13, f32[24,256]{1,0:T(8,128)} %get-tuple-element.1559, f32[256,256]{1,0:T(8,128)S(1)} %fusion.181, pred[256,256]{1,0:T(8,128)(4,1)S(1)} %fusion.182, ...), kind=kOutput, calls=%fused_computation.73.clone.1 | convolution fusion | flops 224835584 | bytes 2154496 | tf_op jit(solution)/shard_map/transpose(jvp())/while/body/eval_jaxpr/checkpoint/hij,jhp->ihp/dot_general | solution.py:55
  269.1 3.9 fusion.189
  289.8 6.2 %fusion.183 = (f32[24,256]{1,0:T(8,128)S(1)}, f32[24,256]{1,0:T(8,128)S(1)}, f32[24,256]{1,0:T(8,128)}, bf16[256,256]{1,0:T(8,128)(2,1)S(1)}) fusion(f32[24,256]{1,0:T(8,128)S(1)} %copy_bitcast_fusion.13, f32[24,256]{1,0:T(8,128)} %get-tuple-element.1559, f32[256,256]{1,0:T(8,128)S(1)} %fusion.181, pred[256,256]{1,0:T(8,128)(4,1)S(1)} %fusion.182, ...), kind=kOutput, calls=%fused_computation.73.clone.1 | convolution fusion | flops 224835584 | bytes 2154496 | tf_op jit(solution)/shard_map/transpose(jvp())/while/body/eval_jaxpr/checkpoint/hij,jhp->ihp/dot_general | solution.py:55
  301.8 3.9 fusion.189
  322.4 6.2 %fusion.183 = (f32[24,256]{1,0:T(8,128)S(1)}, f32[24,256]{1,0:T(8,128)S(1)}, f32[24,256]{1,0:T(8,128)}, bf16[256,256]{1,0:T(8,128)(2,1)S(1)}) fusion(f32[24,256]{1,0:T(8,128)S(1)} %copy_bitcast_fusion.13, f32[24,256]{1,0:T(8,128)} %get-tuple-element.1559, f32[256,256]{1,0:T(8,128)S(1)} %fusion.181, pred[256,256]{1,0:T(8,128)(4,1)S(1)} %fusion.182, ...), kind=kOutput, calls=%fused_computation.73.clone.1 | convolution fusion | flops 224835584 | bytes 2154496 | tf_op jit(solution)/shard_map/transpose(jvp())/while/body/eval_jaxpr/checkpoint/hij,jhp->ihp/dot_general | solution.py:55
  334.4 3.9 fusion.189
  355.0 6.2 %fusion.183 = (f32[24,256]{1,0:T(8,128)S(1)}, f32[24,256]{1,0:T(8,128)S(1)}, f32[24,256]{1,0:T(8,128)}, bf16[256,256]{1,0:T(8,128)(2,1)S(1)}) fusion(f32[24,256]{1,0:T(8,128)S(1)} %copy_bitcast_fusion.13, f32[24,256]{1,0:T(8,128)} %get-tuple-element.1559, f32[256,256]{1,0:T(8,128)S(1)} %fusion.181, pred[256,256]{1,0:T(8,128)(4,1)S(1)} %fusion.182, ...), kind=kOutput, calls=%fused_computation.73.clone.1 | convolution fusion | flops 224835584 | bytes 2154496 | tf_op jit(solution)/shard_map/transpose(jvp())/while/body/eval_jaxpr/checkpoint/hij,jhp->ihp/dot_general | solution.py:55
  367.0 3.9 fusion.189
  376.2 11.6 %while.110 = (s32[]{:T(128)}, f32[24,64,128]{2,1,0:T(8,128)S(1)}, f32[6,24,64,128]{3,2,1,0:T(8,128)}, f32[6,24,1,1]{1,3,2,0:T(1,128)}, s32[]{:T(128)}, /*index=5*/s32[]{:T(128)}, s32[]{:T(128)}) while((s32[]{:T(128)}, f32[24,64,128]{2,1,0:T(8,128)S(1)}, f32[6,24,64,128]{3,2,1,0:T(8,128)}, f32[6,24,1,1]{1,3,2,0:T(1,128)}, ...), condition=%wide.region_33.34_spmd.clone, body=%wide.region_32.33_spmd.clone.sunk | while | flops 589828 | bytes 2359691 | solution.py:42
  393.2 15.2 %while.106 = (s32[]{:T(128)}, f32[24,64,128]{2,1,0:T(8,128)S(1)}, bf16[6,24,64,128]{3,2,1,0:T(8,128)(2,1)S(1)}, f32[6,24]{1,0:T(8,128)S(1)}, f32[6,24,64,128]{3,...) while((s32[]{:T(128)}, f32[24,64,128]{2,1,0:T(8,128)S(1)}, ...), condition=%wide.region_36.37_spmd, body=%wide.region_34.36_spmd.sunk | while | flops 786411 | bytes 4719297 | solution.py:42
  409.9 7.1 %fusion.87 = (f32[6,24,256]{2,1,0:T(8,128)S(1)}, bf16[6,256,128]{1,2,0:T(8,128)(2,1)S(1)}) fusion(f32[6,256,128]{1,2,0:T(8,128)} %copy-done.6, f32[6,24,256]{2,1,0:T(8,128)S(1)} %copy-done.16, bf16[6,24,64,128]{3,2,1,0:T(8,128)(2,1)} %copy-done.4, bf16[6,256,24,64]{1,3,2,0:T(8,128)(2,1)} %get-tuple-element.1777), kind=kOutput, calls=%fused_computation.162 | convolution fusion | flops 627339264 | bytes 8552448 | tf_op jit(solution)/shard_map/transpose(jvp(cjhp,chjn->chpn))/dot_general | solution.py:31
  417.7 14.9 %reduce-window.130 = f32[6,24,2,128]{3,1,2,0:T(8,128)S(1)} reduce-window(f32[6,24,2,128]{3,1,2,0:T(8,128)S(1)} %copy_bitcast_fusion.5, f32[]{:T(128)} %constant.289.clone.1), window={size=1x1x1x128 pad=0_0x0_0x0_0x0_127}, to_apply=%region_40.41 | reduce-window | flops 4681728 | bytes 294916 | tf_op jit(solution)/shard_map/reduce-window.14
  435.3 6.9 %bitcast_add_fusion.6 = bf16[6,256,24,64]{1,3,2,0:T(8,128)(2,1)} fusion(bf16[6,256,24,64]{1,3,2,0:T(8,128)(2,1)} %get-tuple-element.766, bf16[6,24,64,128]{3,2,1,0:T(8,128)(2,1)} %copy-done.4, f32[6,256,128]{1,2,0:T(8,128)S(1)} %copy-done.7, f32[6,24,256]{2,1,0:T(8,128)S(1)} %copy-done.16), kind=kOutput, calls=%fused_computation.171 | convolution fusion | flops 615776256 | bytes 12730368 | tf_op jit(solution)/shard_map/transpose(jvp(cjhp,chjn->chpn))/dot_general | solution.py:31
  442.2 10.4 %copy.250 = bf16[6,256,24,64]{3,2,1,0:T(8,128)(2,1)} copy(bf16[6,256,24,64]{1,3,2,0:T(8,128)(2,1)} %bitcast_add_fusion.6) | data formatting | bytes 9437184
  452.6 13.1 %reshape.633 = bf16[1,1536,1536]{2,1,0:T(8,128)(2,1)} reshape(bf16[6,256,24,64]{3,2,1,0:T(8,128)(2,1)} %copy.250) | data formatting | bytes 9437184
  466.3 62.6 %while.107 = (s32[]{:T(128)}, bf16[6,256,1536]{2,1,0:T(8,128)(2,1)}, bf16[6,256,24,64]{1,3,2,0:T(8,128)(2,1)}, bf16[6,256,256]{2,1,0:T(8,128)(2,1)}, s32[6,256]{...) while((s32[]{:T(128)}, bf16[6,256,1536]{2,1,0:T(8,128)(2,1)}, ...), condition=%wide.region_15.16_spmd.clone, body=%wide.region_10.15_spmd.clone.sunk | while | flops 833433920 | bytes 10981461 | solution.py:79
  472.3 3.5 fusion.167
  492.9 3.6 fusion.167
  513.7 3.6 fusion.167
  524.2 3.5 fusion.167
  529.0 64.8 %all-reduce.5 = (f32[24]{0:T(128)}, f32[24]{0:T(128)}, f32[24]{0:T(128)}) all-reduce(f32[24]{0:T(128)S(1)} %get-tuple-element.1226, f32[24]{0:T(128)S(1)} %add.228, f32[24]{0:T(128)S(1)} %copy-done.26), channel_id=1, replica_groups=mesh['stream'=64,'seq'=2] {'stream','seq'}, use_global_device_ids=true, to_apply=%region_43.44 | all-reduce | flops 72 | bytes 576 | tf_op jit(solution)/shard_map/psum | solution.py:154
  (709 shorter events, 275.9 us)
Async XLA Ops:
  7.2 137.7 %all-gather.3.cloned.1.call-start = ((), (), s32[]{:S(2)}) async-start(), calls=%async_computation | async-start | bytes 25559040 | tf_op jit(solution)/shard_map/all_gather | solution.py:104
  14.3 19.8 %copy-start.32 = (f32[24]{0:T(128)}, f32[24]{0:T(128)S(1)}, u32[]{:S(2)}) copy-start(f32[24]{0:T(128)S(1)} %exp.90) | copy-start | bytes 292
  16.1 29.9 %copy-start.1 = (f32[6,24,256]{2,1,0:T(8,128)}, f32[6,24,256]{2,1,0:T(8,128)S(1)}, u32[]{:S(2)}) copy-start(f32[6,24,256]{2,1,0:T(8,128)S(1)} %get-tuple-element.1738) | copy-start | bytes 442372
  19.9 26.1 %copy-start.11 = (f32[6,24,2]{1,2,0:T(2,128)}, f32[6,24,2]{1,2,0:T(2,128)S(1)}, u32[]{:S(2)}) copy-start(f32[6,24,2]{1,2,0:T(2,128)S(1)} %slice.164) | copy-start | bytes 3460
  21.2 25.0 %copy-start.6 = (f32[6,256,128]{1,2,0:T(8,128)}, f32[6,256,128]{1,2,0:T(8,128)S(1)}, u32[]{:S(2)}) copy-start(f32[6,256,128]{1,2,0:T(8,128)S(1)} %copy.228) | copy-start | bytes 2359300
  34.1 11.9 %copy-start.10 = (f32[24]{0:T(128)S(1)}, f32[24]{0:T(128)}, u32[]{:S(2)}) copy-start(f32[24]{0:T(128)} %param.26) | copy-start | bytes 292
  45.3 8.9 %copy-start.13 = (f32[6,24]{1,0:T(8,128)}, f32[6,24]{1,0:T(8,128)S(1)}, u32[]{:S(2)}) copy-start(f32[6,24]{1,0:T(8,128)S(1)} %slice_reduce_fusion.7) | copy-start | bytes 1732
  46.0 8.2 %copy-start.19 = (pred[6,256]{1,0:T(8,128)(4,1)}, pred[6,256]{1,0:T(8,128)(4,1)S(1)}, u32[]{:S(2)}) copy-start(pred[6,256]{1,0:T(8,128)(4,1)S(1)} %broadcast_compare_fusion.2) | copy-start | bytes 4612
  149.3 4.1 collective-permute-start
  203.9 8.0 %copy-start.21 = (f32[24]{0:T(128)S(1)}, f32[24]{0:T(128)}, u32[]{:S(2)}) copy-start(f32[24]{0:T(128)} %get-tuple-element.1641) | copy-start | bytes 292 | tf_op jit(solution)/shard_map/transpose(jvp())/while
  203.9 8.0 %copy-start.27 = (f32[24]{0:T(128)S(1)}, f32[24]{0:T(128)}, u32[]{:S(2)}) copy-start(f32[24]{0:T(128)} %get-tuple-element.1642) | copy-start | bytes 292 | tf_op jit(solution)/shard_map/transpose(jvp())/while
  236.5 8.0 %copy-start.21 = (f32[24]{0:T(128)S(1)}, f32[24]{0:T(128)}, u32[]{:S(2)}) copy-start(f32[24]{0:T(128)} %get-tuple-element.1641) | copy-start | bytes 292 | tf_op jit(solution)/shard_map/transpose(jvp())/while
  236.5 8.0 %copy-start.27 = (f32[24]{0:T(128)S(1)}, f32[24]{0:T(128)}, u32[]{:S(2)}) copy-start(f32[24]{0:T(128)} %get-tuple-element.1642) | copy-start | bytes 292 | tf_op jit(solution)/shard_map/transpose(jvp())/while
  269.1 8.0 %copy-start.21 = (f32[24]{0:T(128)S(1)}, f32[24]{0:T(128)}, u32[]{:S(2)}) copy-start(f32[24]{0:T(128)} %get-tuple-element.1641) | copy-start | bytes 292 | tf_op jit(solution)/shard_map/transpose(jvp())/while
  269.1 8.0 %copy-start.27 = (f32[24]{0:T(128)S(1)}, f32[24]{0:T(128)}, u32[]{:S(2)}) copy-start(f32[24]{0:T(128)} %get-tuple-element.1642) | copy-start | bytes 292 | tf_op jit(solution)/shard_map/transpose(jvp())/while
  301.7 8.0 %copy-start.27 = (f32[24]{0:T(128)S(1)}, f32[24]{0:T(128)}, u32[]{:S(2)}) copy-start(f32[24]{0:T(128)} %get-tuple-element.1642) | copy-start | bytes 292 | tf_op jit(solution)/shard_map/transpose(jvp())/while
  334.4 8.0 %copy-start.27 = (f32[24]{0:T(128)S(1)}, f32[24]{0:T(128)}, u32[]{:S(2)}) copy-start(f32[24]{0:T(128)} %get-tuple-element.1642) | copy-start | bytes 292 | tf_op jit(solution)/shard_map/transpose(jvp())/while
  367.0 8.0 %copy-start.21 = (f32[24]{0:T(128)S(1)}, f32[24]{0:T(128)}, u32[]{:S(2)}) copy-start(f32[24]{0:T(128)} %get-tuple-element.1641) | copy-start | bytes 292 | tf_op jit(solution)/shard_map/transpose(jvp())/while
  367.0 8.0 %copy-start.27 = (f32[24]{0:T(128)S(1)}, f32[24]{0:T(128)}, u32[]{:S(2)}) copy-start(f32[24]{0:T(128)} %get-tuple-element.1642) | copy-start | bytes 292 | tf_op jit(solution)/shard_map/transpose(jvp())/while
  376.2 11.6 %copy-start.34 = (f32[24]{0:T(128)S(1)}, f32[24]{0:T(128)}, u32[]{:S(2)}) copy-start(f32[24]{0:T(128)} %broadcast_multiply_fusion) | copy-start | bytes 292
  388.8 4.4 collective-permute-start.1
  393.2 15.2 %copy-start.14 = (f32[6,24]{1,0:T(8,128)S(1)}, f32[6,24]{1,0:T(8,128)}, u32[]{:S(2)}) copy-start(f32[6,24]{1,0:T(8,128)} %copy-done.13) | copy-start | bytes 1732
  393.2 15.2 %copy-start.31 = (pred[6]{0:T(512)(128)(4,1)S(1)}, pred[6]{0:T(512)(128)(4,1)}, u32[]{:S(2)}) copy-start(pred[6]{0:T(512)(128)(4,1)} %copy-done.30) | copy-start | bytes 22
  393.2 16.6 %copy-start.16 = (f32[6,24,256]{2,1,0:T(8,128)S(1)}, f32[6,24,256]{2,1,0:T(8,128)}, u32[]{:S(2)}) copy-start(f32[6,24,256]{2,1,0:T(8,128)} %copy-done.15) | copy-start | bytes 442372
  409.8 23.0 %copy-start.33 = (f32[24]{0:T(128)S(1)}, f32[24]{0:T(128)}, u32[]{:S(2)}) copy-start(f32[24]{0:T(128)} %copy-done.32) | copy-start | bytes 292
  409.8 23.4 %copy-start.9 = (f32[6,24,256]{2,1,0:T(8,128)S(1)}, f32[6,24,256]{2,1,0:T(8,128)}, u32[]{:S(2)}) copy-start(f32[6,24,256]{2,1,0:T(8,128)} %get-tuple-element.772) | copy-start | bytes 442372
  409.8 24.2 %copy-start.3 = (bf16[6,256,256]{1,2,0:T(8,128)(2,1)S(1)}, bf16[6,256,256]{1,2,0:T(8,128)(2,1)}, u32[]{:S(2)}) copy-start(bf16[6,256,256]{1,2,0:T(8,128)(2,1)} %get-tuple-element.771) | copy-start | bytes 2359300
  416.9 18.4 %copy-start.7 = (f32[6,256,128]{1,2,0:T(8,128)S(1)}, f32[6,256,128]{1,2,0:T(8,128)}, u32[]{:S(2)}) copy-start(f32[6,256,128]{1,2,0:T(8,128)} %copy-done.6) | copy-start | bytes 2359300
  452.6 13.1 %copy-start.23 = (f32[24]{0:T(128)S(1)}, f32[24]{0:T(128)}, u32[]{:S(2)}) copy-start(f32[24]{0:T(128)} %get-tuple-element.774) | copy-start | bytes 292
  452.6 13.7 %copy-start.35 = (f32[24]{0:T(128)S(1)}, f32[24]{0:T(128)}, u32[]{:S(2)}) copy-start(f32[24]{0:T(128)} %get-tuple-element.1787) | copy-start | bytes 292
  466.3 62.7 %copy-start.29 = (f32[24]{0:T(128)S(1)}, f32[24]{0:T(128)}, u32[]{:S(2)}) copy-start(f32[24]{0:T(128)} %get-tuple-element.775) | copy-start | bytes 292
  466.3 62.7 %copy-start.26 = (f32[24]{0:T(128)S(1)}, f32[24]{0:T(128)}, u32[]{:S(2)}) copy-start(f32[24]{0:T(128)} %get-tuple-element.776) | copy-start | bytes 292
  (62 other events, 269.2 us)
Sparse Core Ops, SparseCore 0:
  10.8 134.0 all-gather.2
where the time goes:
time: 607 us; the launch traced here: 601 us
  local copies, waits for them, and re-layouts  158 us (26%)
  matrix products  151 us (25%)
  other arithmetic  115 us (19%)
  waiting for transfers between devices  86.2 us (14%)
  blocking collectives  67.2 us (11%)
  between operations  16.4 us (3%)
    all_gather x1, waiting for transfers between devices, shards(): gathered = lax.all_gather(old_states, 'stream', axis=0, tiled=True)  82.6 us
    dot_general x18, matrix products, one_group(): jnp.einsum('hij,jhp->ihp', mixing, inputs_q, preferred_element_type=jnp.f...  81.8 us
    psum x1, blocking collectives, shards(): lax.psum((rates_first + rates_second, bias_first + bias_second, skip_tota...  64.8 us
    another operation x80, other arithmetic  52.5 us
    dot_general x24, matrix products, one_group(): jnp.einsum('in,hpn->ihp', c_part.astype(jnp.float32), starts_q, precision...  43.1 us
    unnamed x56, local copies, waits for them, and re-layouts  35.8 us
    squeeze x30, local copies, waits for them, and re-layouts, outputs(): lax.scan(per_group, 0, (inputs_c, maps_c, logits_c, flags_c, starts_c))  22.8 us
    dot_general x3, matrix products, group_states(): jnp.einsum('cjhp,chjn->chpn', inputs_c, b_weighted, preferred_element_typ...  21.9 us
  transfers between devices with their start and end apart: 3, of which 3 were waited for; matrix products, arithmetic and copies ran while one was open for 9% of the time, Pallas kernels for 0%

commit v1 on v0

v1 whole, which is shorter than its diff:
```python
import functools

import jax
import jax.numpy as jnp
from jax import lax
from jax.experimental import pallas as pl
from jax.experimental.pallas import tpu as pltpu
from jax.sharding import PartitionSpec as P

GROUP = 256
LOG2E = 1.4426950408889634
F32 = jnp.float32
BF16 = jnp.bfloat16

NN = (((1,), (0,)), ((), ()))
NT = (((1,), (1,)), ((), ()))


def dot(a, b, dims=NN):
    return lax.dot_general(a, b, dims, preferred_element_type=F32)


def running_sum(v, reverse=False):
    size = v.shape[1]
    lane = lax.broadcasted_iota(jnp.int32, v.shape, 1)
    by = 1
    while by < size:
        if reverse:
            v = v + jnp.where(lane < size - by, pltpu.roll(v, size - by, 1), 0.0)
        else:
            v = v + jnp.where(lane >= by, pltpu.roll(v, by, 1), 0.0)
        by *= 2
    return v


def starts_in(doc_ref, first):
    found = []
    for r in range(doc_ref.shape[1]):
        at = doc_ref[0, r]
        inside = (at >= first) & (at < first + GROUP)
        for q in range(r):
            inside = inside & (doc_ref[0, q] != at)
        found.append((inside.astype(jnp.int32), at))
    return found


def doc_count(found, position):
    total = jnp.zeros(position.shape, jnp.int32)
    for inside, at in found:
        total = total + jnp.where(position >= at, inside, 0)
    return total


def block_terms(logits, heads_ref, found, first):
    shifted = logits + heads_ref[:, 1:2]
    step = jnp.maximum(shifted, 0.0) + jnp.log1p(jnp.exp(-jnp.abs(shifted)))
    rate = jnp.exp(heads_ref[:, 0:1])
    cum = running_sum(-step * rate)
    end = cum[:, GROUP - 1 : GROUP]
    position = first + lax.broadcasted_iota(jnp.int32, (1, GROUP), 1)
    doc = doc_count(found, position)
    docs = sum(inside for inside, _ in found)
    inflow = jnp.where(doc == 0, jnp.exp(cum), 0.0)
    weight = jnp.where(doc == docs, jnp.exp(end - cum), 0.0) * step
    decay = jnp.where(docs == 0, jnp.exp(end), 0.0)
    return shifted, step, rate, cum, doc, inflow, weight, decay


def first_kernel(
    heads,
    head_dim,
    doc_ref,
    base_ref,
    x_ref,
    dy_ref,
    maps_ref,
    logits_ref,
    heads_ref,
    xt_ref,
    dyt_ref,
    states_ref,
    after_ref,
    suffix_ref,
    local_ref,
    grad_ref,
    total_ref,
    weight_s,
    inflow_s,
    decay_s,
):
    step_id = pl.program_id(0)
    block = pl.num_programs(0) - 1 - step_id
    first = base_ref[0, 0] + block * GROUP
    state_n = maps_ref.shape[1] // 2

    @pl.when(step_id == 0)
    def _():
        local_ref[...] = jnp.zeros_like(local_ref)
        grad_ref[...] = jnp.zeros_like(grad_ref)
        total_ref[...] = jnp.ones_like(total_ref)

    found = starts_in(doc_ref, first)
    _, _, _, _, _, inflow, weight, decay = block_terms(logits_ref[...], heads_ref, found, first)
    weight_s[...] = weight
    inflow_s[...] = inflow
    decay_s[...] = jnp.broadcast_to(decay, decay_s.shape)
    suffix_ref[...] = total_ref[...]
    b_part = maps_ref[:, :state_n]
    c_part = maps_ref[:, state_n:]

    def pair(k, _):
        cols = pl.ds(pl.multiple_of(k * 2 * head_dim, 2 * head_dim), 2 * head_dim)
        xt_ref[cols, :] = x_ref[:, cols].T
        dyt_ref[cols, :] = dy_ref[:, cols].T
        for one in range(2):
            h = k * 2 + one
            rows = pl.ds(pl.multiple_of(h * head_dim, head_dim), head_dim)
            head = pl.ds(h, 1)
            xw = (xt_ref[rows, :].astype(F32) * weight_s[head, :]).astype(BF16)
            dyi = (dyt_ref[rows, :].astype(F32) * inflow_s[head, :]).astype(BF16)
            state = dot(xw, b_part)
            grad = dot(dyi, c_part)
            states_ref[rows, :] = state
            after = grad_ref[rows, :]
            after_ref[rows, :] = after
            local_ref[rows, :] += total_ref[head, :] * state
            grad_ref[rows, :] = decay_s[head, :] * after + grad
        return 0

    lax.fori_loop(0, heads // 2, pair, 0)
    total_ref[...] = total_ref[...] * decay_s[...]


def first_pass(doc, base, x, dy, maps, logits, head_params):
    length, width = x.shape
    heads = logits.shape[0]
    state_n = maps.shape[1] // 2
    groups = length // GROUP
    back = lambda i: groups - 1 - i
    smem = pl.BlockSpec(memory_space=pltpu.SMEM)
    per_block = lambda rows, cols: pl.BlockSpec((None, rows, cols), lambda i: (back(i), 0, 0))
    whole = lambda rows, cols: pl.BlockSpec((rows, cols), lambda i: (0, 0))
    return pl.pallas_call(
        functools.partial(first_kernel, heads, width // heads),
        grid=(groups,),
        in_specs=[
            smem,
            smem,
            pl.BlockSpec((GROUP, width), lambda i: (back(i), 0)),
            pl.BlockSpec((GROUP, width), lambda i: (back(i), 0)),
            pl.BlockSpec((GROUP, 2 * state_n), lambda i: (back(i), 0)),
            pl.BlockSpec((heads, GROUP), lambda i: (0, back(i))),
            whole(heads, head_params.shape[1]),
        ],
        out_specs=[
            per_block(width, GROUP),
            per_block(width, GROUP),
            per_block(width, state_n),
            per_block(width, state_n),
            per_block(heads, state_n),
            whole(width, state_n),
            whole(width, state_n),
            whole(heads, state_n),
        ],
        out_shape=[
            jax.ShapeDtypeStruct((groups, width, GROUP), BF16),
            jax.ShapeDtypeStruct((groups, width, GROUP), BF16),
            jax.ShapeDtypeStruct((groups, width, state_n), F32),
            jax.ShapeDtypeStruct((groups, width, state_n), F32),
            jax.ShapeDtypeStruct((groups, heads, state_n), F32),
            jax.ShapeDtypeStruct((width, state_n), F32),
            jax.ShapeDtypeStruct((width, state_n), F32),
            jax.ShapeDtypeStruct((heads, state_n), F32),
        ],
        scratch_shapes=[
            pltpu.VMEM((heads, GROUP), F32),
            pltpu.VMEM((heads, GROUP), F32),
            pltpu.VMEM((heads, state_n), F32),
        ],
        compiler_params=pltpu.CompilerParams(
            dimension_semantics=("arbitrary",), vmem_limit_bytes=48 << 20
        ),
        cost_estimate=pl.CostEstimate(
            flops=4 * length * width * state_n,
            bytes_accessed=8 * length * width + 8 * groups * width * state_n,
            transcendentals=4 * heads * length,
        ),
        name="first_pass",
    )(doc, base, x, dy, maps, logits, head_params)


def second_kernel(
    heads,
    head_dim,
    doc_ref,
    base_ref,
    skip_ref,
    x_ref,
    xt_ref,
    dyt_ref,
    maps_ref,
    logits_ref,
    heads_ref,
    states_ref,
    after_ref,
    suffix_ref,
    entry_ref,
    exit_ref,
    y_ref,
    dx_ref,
    dmaps_ref,
    dlogits_ref,
    sums_ref,
    start_s,
    weight_s,
    inflow_s,
    decay_s,
    over_s,
    under_s,
    scores_s,
    dscores_s,
    mix_s,
    start_t,
    after_t,
    xw_s,
    dyi_s,
    out_s,
    in_s,
    skip_s,
    ends_s,
):
    block = pl.program_id(0)
    first = base_ref[0, 0] + block * GROUP
    state_n = maps_ref.shape[1] // 2
    half = GROUP // 2

    @pl.when(block == 0)
    def _():
        start_s[...] = entry_ref[...]
        sums_ref[...] = jnp.zeros_like(sums_ref)
        mix_s[...] = jnp.zeros_like(mix_s)

    found = starts_in(doc_ref, first)
    shifted, step, rate, cum, doc, inflow, weight, decay = block_terms(
        logits_ref[...], heads_ref, found, first
    )
    weight_s[...] = weight
    inflow_s[...] = inflow
    decay_s[...] = jnp.broadcast_to(decay, decay_s.shape)
    over = cum * LOG2E
    over_s[...] = over
    under = over - jnp.log2(step)
    pad = jnp.zeros((half - heads, GROUP), F32)
    under_t = jnp.concatenate([under, pad], axis=0).T
    for h in range(heads):
        under_s[h] = jnp.broadcast_to(under_t[:, h : h + 1], (GROUP, half))

    b_part = maps_ref[:, :state_n]
    c_part = maps_ref[:, state_n:]
    b_t = b_part.T
    c_t = c_part.T
    j_at = lax.broadcasted_iota(jnp.int32, (GROUP, GROUP), 0)
    i_at = lax.broadcasted_iota(jnp.int32, (GROUP, GROUP), 1)
    j_doc = doc_count(found, first + lax.broadcasted_iota(jnp.int32, (GROUP, GROUP), 0))
    visible = (j_at <= i_at) & (j_doc == doc)
    scores_s[...] = jnp.where(visible, dot(b_part, c_t), 0.0)
    dscores_s[...] = jnp.zeros_like(dscores_s)

    def pair(k, _):
        cols = pl.ds(pl.multiple_of(k * 2 * head_dim, 2 * head_dim), 2 * head_dim)
        start = start_s[cols, :]
        start_b = start.astype(BF16)
        start_t[:, cols] = start_b.T
        carried = dot(start_b, c_t)
        pair_suffix = []
        next_parts = []
        for one in range(2):
            h = k * 2 + one
            head = pl.ds(h, 1)
            rows = pl.ds(pl.multiple_of(h * head_dim, head_dim), head_dim)
            lo = one * head_dim
            after = suffix_ref[head, :] * exit_ref[rows, :] + after_ref[rows, :]
            pair_suffix.append(after)
            new = decay_s[head, :] * start[lo : lo + head_dim, :] + states_ref[rows, :]
            next_parts.append(new)
            ends_s[head, :] = jnp.sum(new * after, axis=0, keepdims=True)
        start_s[cols, :] = jnp.concatenate(next_parts, axis=0)
        after_b = jnp.concatenate(pair_suffix, axis=0).astype(BF16)
        after_t[:, cols] = after_b.T
        given = dot(after_b, b_t)
        x_pair = x_ref[:, cols]
        for one in range(2):
            h = k * 2 + one
            head = pl.ds(h, 1)
            rows = pl.ds(pl.multiple_of(h * head_dim, head_dim), head_dim)
            lo = one * head_dim
            xt = xt_ref[rows, :]
            dyt = dyt_ref[rows, :]
            zero = jnp.zeros_like(dyt)
            dyt_wide = jnp.concatenate([dyt, zero] if one == 0 else [zero, dyt], axis=0)
            over_h = over_s[head, :]
            for lo_j, lo_i in ((0, 0), (half, half)):
                js = pl.ds(lo_j, half)
                dmix = dot(x_pair[lo_j : lo_j + half, :], dyt_wide[:, lo_i:])
                for at in range(lo_i, GROUP, half):
                    ins = pl.ds(at, half)
                    gap = over_h[:, at : at + half] - under_s[h, js, :]
                    if at == lo_j:
                        gap = jnp.minimum(gap, 64.0)
                    shape = jnp.exp2(gap)
                    mix_s[one, js, ins] = (scores_s[js, ins] * shape).astype(BF16)
                    dscores_s[js, ins] += dmix[:, at - lo_i : at - lo_i + half] * shape
            mix = mix_s[one]
            x32 = xt.astype(F32)
            dy32 = dyt.astype(F32)
            skip = skip_ref[h]
            inflow_h = inflow_s[head, :]
            weight_h = weight_s[head, :]
            xw_s[rows, :] = (x32 * weight_h).astype(BF16)
            dyi_s[rows, :] = (dy32 * inflow_h).astype(BF16)
            y = dot(xt, mix) + carried[lo : lo + head_dim, :] * inflow_h
            out_s[head, :] = jnp.sum(dy32 * y, axis=0, keepdims=True)
            skip_s[head, :] = jnp.sum(dy32 * x32, axis=0, keepdims=True)
            y_t = (y + skip * x32).astype(BF16)
            dx = dot(dyt, mix, NT) + given[lo : lo + head_dim, :] * weight_h
            in_s[head, :] = jnp.sum(x32 * dx, axis=0, keepdims=True)
            dx_t = (dx + skip * dy32).astype(BF16)
            if one == 0:
                kept = (y_t, dx_t)
            else:
                y_ref[:, cols] = jnp.concatenate([kept[0], y_t], axis=0).T
                dx_ref[:, cols] = jnp.concatenate([kept[1], dx_t], axis=0).T
        return 0

    lax.fori_loop(0, heads // 2, pair, 0)

    dscores = jnp.where(visible, dscores_s[...], 0.0).astype(BF16)
    dc_t = dot(start_t[...], dyi_s[...]) + dot(b_t, dscores)
    db_t = dot(after_t[...], xw_s[...]) + dot(c_t, dscores, NT)
    dmaps_ref[:, :state_n] = db_t.T.astype(BF16)
    dmaps_ref[:, state_n:] = dc_t.T.astype(BF16)

    lane = lax.broadcasted_iota(jnp.int32, (heads, GROUP), 1)
    ends = jnp.sum(ends_s[...], axis=1, keepdims=True)
    inner = in_s[...]
    dcum = out_s[...] - inner + jnp.where(lane == GROUP - 1, ends, 0.0)
    dlog = running_sum(dcum, reverse=True)
    dstep = inner / step - rate * dlog
    dlogits = dstep * jax.nn.sigmoid(shifted)
    dlogits_ref[...] = dlogits
    sums_ref[0] += -step * rate * dlog
    sums_ref[1] += dlogits
    sums_ref[2] += skip_s[...]


def second_pass(
    doc, base, skip_gain, x, xt, dyt, maps, logits, head_params, states, after, suffix, entry, leave
):
    length, width = x.shape
    heads = logits.shape[0]
    state_n = maps.shape[1] // 2
    groups = length // GROUP
    half = GROUP // 2
    smem = pl.BlockSpec(memory_space=pltpu.SMEM)
    per_block = lambda rows, cols: pl.BlockSpec((None, rows, cols), lambda i: (i, 0, 0))
    whole = lambda rows, cols: pl.BlockSpec((rows, cols), lambda i: (0, 0))
    return pl.pallas_call(
        functools.partial(second_kernel, heads, width // heads),
        grid=(groups,),
        in_specs=[
            smem,
            smem,
            smem,
            pl.BlockSpec((GROUP, width), lambda i: (i, 0)),
            per_block(width, GROUP),
            per_block(width, GROUP),
            pl.BlockSpec((GROUP, 2 * state_n), lambda i: (i, 0)),
            pl.BlockSpec((heads, GROUP), lambda i: (0, i)),
            whole(heads, head_params.shape[1]),
            per_block(width, state_n),
            per_block(width, state_n),
            per_block(heads, state_n),
            whole(width, state_n),
            whole(width, state_n),
        ],
        out_specs=[
            pl.BlockSpec((GROUP, width), lambda i: (i, 0)),
            pl.BlockSpec((GROUP, width), lambda i: (i, 0)),
            pl.BlockSpec((GROUP, 2 * state_n), lambda i: (i, 0)),
            pl.BlockSpec((heads, GROUP), lambda i: (0, i)),
            pl.BlockSpec((3, heads, GROUP), lambda i: (0, 0, 0)),
        ],
        out_shape=[
            jax.ShapeDtypeStruct((length, width), BF16),
            jax.ShapeDtypeStruct((length, width), BF16),
            jax.ShapeDtypeStruct((length, 2 * state_n), BF16),
            jax.ShapeDtypeStruct((heads, length), F32),
            jax.ShapeDtypeStruct((3, heads, GROUP), F32),
        ],
        scratch_shapes=[
            pltpu.VMEM((width, state_n), F32),
            pltpu.VMEM((heads, GROUP), F32),
            pltpu.VMEM((heads, GROUP), F32),
            pltpu.VMEM((heads, state_n), F32),
            pltpu.VMEM((heads, GROUP), F32),
            pltpu.VMEM((heads, GROUP, half), F32),
            pltpu.VMEM((GROUP, GROUP), F32),
            pltpu.VMEM((GROUP, GROUP), F32),
            pltpu.VMEM((2, GROUP, GROUP), BF16),
            pltpu.VMEM((state_n, width), BF16),
            pltpu.VMEM((state_n, width), BF16),
            pltpu.VMEM((width, GROUP), BF16),
            pltpu.VMEM((width, GROUP), BF16),
            pltpu.VMEM((heads, GROUP), F32),
            pltpu.VMEM((heads, GROUP), F32),
            pltpu.VMEM((heads, GROUP), F32),
            pltpu.VMEM((heads, state_n), F32),
        ],
        compiler_params=pltpu.CompilerParams(
            dimension_semantics=("arbitrary",), vmem_limit_bytes=56 << 20
        ),
        cost_estimate=pl.CostEstimate(
            flops=groups * heads * GROUP * (6 * GROUP * 64 + 8 * 64 * state_n),
            bytes_accessed=10 * length * width + 8 * groups * width * state_n,
            transcendentals=heads * length * GROUP,
        ),
        name="second_pass",
    )(doc, base, skip_gain, x, xt, dyt, maps, logits, head_params, states, after, suffix, entry, leave)


def sent_to_successor(block, owner):
    streams = lax.axis_size("stream")
    pieces = block.reshape(streams, -1)
    dealt = lax.all_to_all(pieces, "stream", 0, 0, tiled=True)
    chosen = jnp.take(dealt, owner, axis=0)
    return lax.all_to_all(chosen, "stream", 0, 0, tiled=True).reshape(block.shape)


def shards(
    head_inputs,
    state_maps,
    step_logits,
    log_rates,
    step_bias,
    skip_gain,
    old_states,
    old_owner,
    doc_starts,
    grad_output,
):
    length, width = head_inputs.shape[1:]
    heads = step_logits.shape[1]
    state_n = old_states.shape[3]
    head_dim = old_states.shape[2]
    seq_index = lax.axis_index("seq")
    is_first = seq_index == 0
    swap = [(0, 1), (1, 0)]
    base = (seq_index * length).astype(jnp.int32).reshape(1, 1)
    head_params = jnp.stack([log_rates, step_bias], axis=1)

    own = sent_to_successor(old_states[0], old_owner).reshape(width // 2, state_n)

    x, dy, maps, logits = head_inputs[0], grad_output[0], state_maps[0], step_logits[0]
    xt, dyt, states, after, suffix, local, grad, total = first_pass(
        doc_starts, base, x, dy, maps, logits, head_params
    )
    other = lax.ppermute(own, "seq", swap)
    start = jnp.where(
        is_first, jnp.concatenate([own, other], axis=0), jnp.concatenate([other, own], axis=0)
    )
    scaled = (total[:, None, :] * start.reshape(heads, head_dim, state_n)).reshape(width, state_n)
    sent = jnp.where(is_first, scaled + local, grad)
    received = lax.ppermute(sent, "seq", swap)
    entry = jnp.where(is_first, start, received)
    leave = jnp.where(is_first, received, 0.0)
    y, dx, dmaps, dlogits, sums = second_pass(
        doc_starts, base, skip_gain, x, xt, dyt, maps, logits, head_params,
        states, after, suffix, entry, leave,
    )
    totals = jnp.sum(sums, axis=2)
    totals = totals + lax.ppermute(totals, "seq", swap)
    streams = lax.axis_size("stream")
    by = 1
    while by < streams:
        totals = totals + lax.ppermute(totals, "stream", [(s, s ^ by) for s in range(streams)])
        by *= 2
    return (y[None], dx[None], dmaps[None], dlogits[None], totals[0], totals[1], totals[2])


def solution(mesh):
    return jax.shard_map(
        shards,
        mesh=mesh,
        in_specs=(
            P("stream", "seq", None),
            P("stream", "seq", None),
            P("stream", None, "seq"),
            P(),
            P(),
            P(),
            P("stream", "seq", None, None),
            P(),
            P("stream", None),
            P("stream", "seq", None),
        ),
        out_specs=(
            P("stream", "seq", None),
            P("stream", "seq", None),
            P("stream", "seq", None),
            P("stream", None, "seq"),
            P(),
            P(),
            P(),
        ),
        check_vma=False,
    )
```

time: 607 us -> 149 us (0.25); the launches traced: 601 us -> 149 us
  local copies, waits for them, and re-layouts: 158 us -> 2.12 us
  matrix products: 151 us -> 0 us
  other arithmetic: 115 us -> 3.99 us
  Pallas kernels: 0 us -> 74.3 us
  blocking collectives: 67.2 us -> 15.9 us
  waiting for transfers between devices: 86.2 us -> 35.3 us
  between operations: 16.4 us -> 0.76 us
  starting transfers between devices: 3.8 us -> 16.7 us
    dot_general x69 -> x0, matrix products: 151 us -> none  [the longest x18 81.8 us: one_group(): jnp.einsum('hij,jhp->ihp', mixing, inputs_q, preferred_element_type=jnp.f...]
    all_gather x1 -> x0, waiting for transfers between devices: 82.6 us -> none  [shards(): gathered = lax.all_gather(old_states, 'stream', axis=0, tiled=True)]
    pallas_call x0 -> x2, Pallas kernels: none -> 74.3 us  [the longest x1 49.7 us: second_pass(): pl.pallas_call(functools.partial(second_kernel, heads, width // heads), g...]
    psum x1 -> x0, blocking collectives: 64.8 us -> none  [shards(): lax.psum((rates_first + rates_second, bias_first + bias_second, skip_tota...]
    another operation x80 -> x1, other arithmetic: 52.5 us -> 0.01 us  [shards(): head_params = jnp.stack([log_rates, step_bias], axis=1)]
    unnamed x56 -> x15, local copies, waits for them, and re-layouts: 35.8 us -> 0.39 us
    squeeze x36 -> x1, local copies, waits for them, and re-layouts: 29.9 us -> 0.52 us  [shards(): totals[2]]
    another operation x86 -> x1, local copies, waits for them, and re-layouts: 25.5 us -> 0.09 us  [shards(): head_params = jnp.stack([log_rates, step_bias], axis=1)]
  transfers between devices with their start and end apart: 3 -> 10, of which waited for: 3 -> 9; matrix products, arithmetic and copies ran while one was open for 9% -> 1% of each run, Pallas kernels for 0% -> 16%
where the time goes in v1:
time: 149 us
  Pallas kernels  74.3 us (50%)
  waiting for transfers between devices  35.3 us (24%)
  starting transfers between devices  16.7 us (11%)
  blocking collectives  15.9 us (11%)
  other arithmetic  3.99 us (3%)
  local copies, waits for them, and re-layouts  2.12 us (1%)
    pallas_call x1, Pallas kernels, second_pass(): pl.pallas_call(functools.partial(second_kernel, heads, width // heads), g...  49.7 us
    pallas_call x1, Pallas kernels, first_pass(): pl.pallas_call(functools.partial(first_kernel, heads, width // heads), gr...  24.6 us
    ppermute x6, waiting for transfers between devices, shards(): lax.ppermute(totals, 'stream', [(s, s ^ by) for s in range(streams)])  21.9 us
    all_to_all x1, blocking collectives, sent_to_successor(): lax.all_to_all(chosen, 'stream', 0, 0, tiled=True).reshape(block.shape)  15.9 us
    all_to_all x1, starting transfers between devices, sent_to_successor(): dealt = lax.all_to_all(pieces, 'stream', 0, 0, tiled=True)  11.6 us
    all_to_all x1, waiting for transfers between devices, sent_to_successor(): dealt = lax.all_to_all(pieces, 'stream', 0, 0, tiled=True)  10.6 us
    ppermute x6, starting transfers between devices, shards(): lax.ppermute(totals, 'stream', [(s, s ^ by) for s in range(streams)])  4.09 us
  transfers between devices with their start and end apart: 10, of which 9 were waited for; matrix products, arithmetic and copies ran while one was open for 1% of the time, Pallas kernels for 16%

profile of v1, /device:TPU:0, one launch (start us, length us, event | category | flops | bytes accessed | tf_op | source)
XLA Modules:
  0.0 149.0 jit_solution(11839830853283376392)
XLA Ops:
  0.7 11.6 %all-to-all-start = ((f32[64,1,1536]{2,1,0:T(1,128)}), f32[64,1,1536]{2,1,0:T(1,128)S(1)}, u32[]{:S(2)}, u32[]{:S(2)}) async-start(f32[64,1,1536]{2,1,0:T(1,128)} %bitcast.41), calls=%async_computation | async-start | bytes 786432 | tf_op jit(solution)/shard_map/all_to_all | solution.py:434
  12.3 0.7 compare_select_fusion
  13.0 0.7 compare_and_fusion
  13.7 10.6 %all-to-all-done = f32[64,1,1536]{2,1,0:T(1,128)S(1)} async-done(((f32[64,1,1536]{2,1,0:T(1,128)}), f32[64,1,1536]{2,1,0:T(1,128)S(1)}, u32[]{:S(2)}, u32[]{:S(2)}) %all-to-all-start) | async-done | bytes 393248 | tf_op jit(solution)/shard_map/all_to_all | solution.py:434
  24.3 0.7 gather_fusion
  25.1 0.1 bitcast_select_fusion
  25.2 0.4 copy.20
  25.6 15.9 %all_to_all.18 = f32[64,1,1536]{2,1,0:T(1,128)S(1)} all-to-all(f32[64,1,1536]{2,1,0:T(1,128)S(1)} %copy.20), channel_id=1, replica_groups=mesh['stream'=64,'seq'=2] {'stream'}, dimensions={0} | all-to-all | bytes 786432 | tf_op jit(solution)/shard_map/all_to_all | solution.py:436
  41.5 0.1 copy.19.heads_ref
  41.6 24.6 %first_pass.1 = (bf16[6,1536,256]{2,1,0:T(8,128)(2,1)}, bf16[6,1536,256]{2,1,0:T(8,128)(2,1)}, f32[6,1536,128]{2,1,0:T(8,128)}, f32[6,1536,128]{2,1,0:T(8,128)},...) custom-call(s32[1,2]{1,0:T(1,128)S(1)} %copy-done.4, ...), custom_call_target="tpu_custom_call" | custom-call | flops 1207959552 | bytes 28311552 | tf_op jit(solution)/shard_map/first_pass/pallas_call | solution.py:143
  66.2 0.3 fusion.1
  66.5 0.3 copy-done.3
  66.8 0.5 collective-permute-start.1
  67.3 1.9 %collective-permute-done.1 = f32[1536,128]{1,0:T(8,128)S(1)} collective-permute-done((f32[1536,128]{1,0:T(8,128)S(1)}, f32[1536,128]{1,0:T(8,128)S(1)}, u32[]{:S(2)}, u32[]{:S(2)}) %collective-permute-start.1) | collective-permute-done | bytes 786464 | tf_op jit(solution)/shard_map/ppermute | solution.py:473
  69.2 1.3 broadcast_select_fusion
  70.5 49.7 %second_pass.1 = (bf16[1536,1536]{1,0:T(8,128)(2,1)}, bf16[1536,1536]{1,0:T(8,128)(2,1)}, bf16[1536,256]{1,0:T(8,128)(2,1)}, f32[24,1536]{1,0:T(8,128)}, f32[3,24,256]{2,1,0:T(8,128)}) custom-call(s32[1,2]{1,0:T(1,128)} %doc_ref.3, s32[1,1]{1,0:T(1,128)} %bitcast.base_ref, f32[24]{0:T(128)} %skip_ref.1, bf16[1536,1536]{1,0:T(8,128)(2,1)} %bitcast.36, ...), custom_call_target="tpu_custom_call" | custom-call | flops 6039797760 | bytes 33030144 | tf_op jit(solution)/shard_map/second_pass/pallas_call | solution.py:367
  120.2 1.0 reduce_sum.9
  121.2 0.5 collective-permute-start.2
  121.6 0.8 collective-permute-done.2
  122.4 0.6 collective-permute-start.3
  123.0 3.0 %collective-permute-done.3 = f32[3,24]{1,0:T(4,128)S(1)} collective-permute-done((f32[3,24]{1,0:T(4,128)S(1)}, f32[3,24]{1,0:T(4,128)S(1)}, u32[]{:S(2)}, u32[]{:S(2)}) %collective-permute-start.3) | collective-permute-done | bytes 320 | tf_op jit(solution)/shard_map/ppermute | solution.py:485
  126.0 1.2 collective-permute-start.4
  127.2 3.9 %collective-permute-done.4 = f32[3,24]{1,0:T(4,128)S(1)} collective-permute-done((f32[3,24]{1,0:T(4,128)S(1)}, f32[3,24]{1,0:T(4,128)S(1)}, u32[]{:S(2)}, u32[]{:S(2)}) %collective-permute-start.4) | collective-permute-done | bytes 320 | tf_op jit(solution)/shard_map/ppermute | solution.py:485
  131.1 0.6 collective-permute-start.5
  131.7 3.0 %collective-permute-done.5 = f32[3,24]{1,0:T(4,128)S(1)} collective-permute-done((f32[3,24]{1,0:T(4,128)S(1)}, f32[3,24]{1,0:T(4,128)S(1)}, u32[]{:S(2)}, u32[]{:S(2)}) %collective-permute-start.5) | collective-permute-done | bytes 320 | tf_op jit(solution)/shard_map/ppermute | solution.py:485
  134.7 0.6 collective-permute-start.6
  135.3 4.5 %collective-permute-done.6 = f32[3,24]{1,0:T(4,128)S(1)} collective-permute-done((f32[3,24]{1,0:T(4,128)S(1)}, f32[3,24]{1,0:T(4,128)S(1)}, u32[]{:S(2)}, u32[]{:S(2)}) %collective-permute-start.6) | collective-permute-done | bytes 320 | tf_op jit(solution)/shard_map/ppermute | solution.py:485
  139.8 0.5 collective-permute-start.7
  140.3 3.1 %collective-permute-done.7 = f32[3,24]{1,0:T(4,128)S(1)} collective-permute-done((f32[3,24]{1,0:T(4,128)S(1)}, f32[3,24]{1,0:T(4,128)S(1)}, u32[]{:S(2)}, u32[]{:S(2)}) %collective-permute-start.7) | collective-permute-done | bytes 320 | tf_op jit(solution)/shard_map/ppermute | solution.py:485
  143.4 0.6 collective-permute-start.8
  144.0 4.5 %collective-permute-done.8 = f32[3,24]{1,0:T(4,128)S(1)} collective-permute-done((f32[3,24]{1,0:T(4,128)S(1)}, f32[3,24]{1,0:T(4,128)S(1)}, u32[]{:S(2)}, u32[]{:S(2)}) %collective-permute-start.8) | collective-permute-done | bytes 320 | tf_op jit(solution)/shard_map/ppermute | solution.py:485
  148.5 0.5 slice_bitcast_fusion
  (25 shorter events, 0.1 us)
Async XLA Ops:
  0.6 40.8 %copy-start.5 = (f32[24]{0:T(128)S(1)}, f32[24]{0:T(128)}, u32[]{:S(2)}) copy-start(f32[24]{0:T(128)} %param.14) | copy-start | bytes 292
  0.6 40.8 %copy-start.6 = (f32[24]{0:T(128)S(1)}, f32[24]{0:T(128)}, u32[]{:S(2)}) copy-start(f32[24]{0:T(128)} %param.13) | copy-start | bytes 292
  0.7 40.9 %copy-start.4 = (s32[1,2]{1,0:T(1,128)S(1)}, s32[1,2]{1,0:T(1,128)}, u32[]{:S(2)}) copy-start(s32[1,2]{1,0:T(1,128)} %doc_ref.3) | copy-start | bytes 28
  0.7 40.9 %copy-start.1 = (f32[1,24,1536]{2,1,0:T(8,128)S(1)}, f32[1,24,1536]{2,1,0:T(8,128)}, u32[]{:S(2)}) copy-start(f32[1,24,1536]{2,1,0:T(8,128)} %param.12) | copy-start | bytes 442372
  0.7 40.9 %copy-start = (bf16[1,1536,256]{2,1,0:T(8,128)(2,1)S(1)}, bf16[1,1536,256]{2,1,0:T(8,128)(2,1)}, u32[]{:S(2)}) copy-start(bf16[1,1536,256]{2,1,0:T(8,128)(2,1)} %param.11) | copy-start | bytes 2359300
  0.7 23.6 %all-to-all-start = ((f32[64,1,1536]{2,1,0:T(1,128)}), f32[64,1,1536]{2,1,0:T(1,128)S(1)}, u32[]{:S(2)}, u32[]{:S(2)}) async-start(f32[64,1,1536]{2,1,0:T(1,128)} %bitcast.41), calls=%async_computation | async-start | bytes 786432 | tf_op jit(solution)/shard_map/all_to_all | solution.py:434
  41.5 24.7 %collective-permute-start = (f32[768,128]{1,0:T(8,128)S(1)}, f32[768,128]{1,0:T(8,128)S(1)}, u32[]{:S(2)}, u32[]{:S(2)}) collective-permute-start(f32[768,128]{1,0:T(8,128)S(1)} %bitcast.38), channel_id=1, source_target_pairs={{0,1},{1,0},{2,3},{3,2},{4,5},{5,4},{6,7},{7,6},{8,9},{9,8},{10,11... | collective-permute-start | bytes 1179656 | tf_op jit(solution)/shard_map/ppermute | solution.py:467
  41.6 24.6 %copy-start.2 = (f32[24,2]{1,0:T(8,128)}, f32[24,2]{1,0:T(8,128)S(1)}, u32[]{:S(2)}) copy-start(f32[24,2]{1,0:T(8,128)S(1)} %copy.19.heads_ref) | copy-start | bytes 580
  66.2 0.6 copy-start.3
  66.8 2.4 %collective-permute-start.1 = (f32[1536,128]{1,0:T(8,128)S(1)}, f32[1536,128]{1,0:T(8,128)S(1)}, u32[]{:S(2)}, u32[]{:S(2)}) collective-permute-start(f32[1536,128]{1,0:T(8,128)S(1)} %fusion.1), channel_id=1, source_target_pairs={{0,1},{1,0},{2,3},{3,2},{4,5},{5,4},{6,7},{7,6},{8,9},{9,8},{10,11... | collective-permute-start | bytes 2359304 | tf_op jit(solution)/shard_map/ppermute | solution.py:473
  121.2 1.3 collective-permute-start.2
  122.4 3.6 %collective-permute-start.3 = (f32[3,24]{1,0:T(4,128)S(1)}, f32[3,24]{1,0:T(4,128)S(1)}, u32[]{:S(2)}, u32[]{:S(2)}) collective-permute-start(f32[3,24]{1,0:T(4,128)S(1)} %add.35), channel_id=1, source_target_pairs={{0,2},{2,0},{4,6},{6,4},{8,10},{10,8},{12,14},{14,12},{16,18},{18,... | collective-permute-start | bytes 872 | tf_op jit(solution)/shard_map/ppermute | solution.py:485
  126.0 5.1 %collective-permute-start.4 = (f32[3,24]{1,0:T(4,128)S(1)}, f32[3,24]{1,0:T(4,128)S(1)}, u32[]{:S(2)}, u32[]{:S(2)}) collective-permute-start(f32[3,24]{1,0:T(4,128)S(1)} %add.36), channel_id=1, source_target_pairs={{0,4},{2,6},{4,0},{6,2},{8,12},{10,14},{12,8},{14,10},{16,20},{18,... | collective-permute-start | bytes 872 | tf_op jit(solution)/shard_map/ppermute | solution.py:485
  131.1 3.6 %collective-permute-start.5 = (f32[3,24]{1,0:T(4,128)S(1)}, f32[3,24]{1,0:T(4,128)S(1)}, u32[]{:S(2)}, u32[]{:S(2)}) collective-permute-start(f32[3,24]{1,0:T(4,128)S(1)} %add.37), channel_id=1, source_target_pairs={{0,8},{2,10},{4,12},{6,14},{8,0},{10,2},{12,4},{14,6},{16,24},{18,... | collective-permute-start | bytes 872 | tf_op jit(solution)/shard_map/ppermute | solution.py:485
  134.7 5.1 %collective-permute-start.6 = (f32[3,24]{1,0:T(4,128)S(1)}, f32[3,24]{1,0:T(4,128)S(1)}, u32[]{:S(2)}, u32[]{:S(2)}) collective-permute-start(f32[3,24]{1,0:T(4,128)S(1)} %add.38), channel_id=1, source_target_pairs={{0,16},{2,18},{4,20},{6,22},{8,24},{10,26},{12,28},{14,30},{16,0},... | collective-permute-start | bytes 872 | tf_op jit(solution)/shard_map/ppermute | solution.py:485
  139.8 3.6 %collective-permute-start.7 = (f32[3,24]{1,0:T(4,128)S(1)}, f32[3,24]{1,0:T(4,128)S(1)}, u32[]{:S(2)}, u32[]{:S(2)}) collective-permute-start(f32[3,24]{1,0:T(4,128)S(1)} %add.39), channel_id=1, source_target_pairs={{0,32},{2,34},{4,36},{6,38},{8,40},{10,42},{12,44},{14,46},{16,48}... | collective-permute-start | bytes 872 | tf_op jit(solution)/shard_map/ppermute | solution.py:485
  143.4 5.1 %collective-permute-start.8 = (f32[3,24]{1,0:T(4,128)S(1)}, f32[3,24]{1,0:T(4,128)S(1)}, u32[]{:S(2)}, u32[]{:S(2)}) collective-permute-start(f32[3,24]{1,0:T(4,128)S(1)} %add.40), channel_id=1, source_target_pairs={{0,64},{2,66},{4,68},{6,70},{8,72},{10,74},{12,76},{14,78},{16,80}... | collective-permute-start | bytes 872 | tf_op jit(solution)/shard_map/ppermute | solution.py:485

commit v2 on v1

--- a/solution.py
+++ b/solution.py
@@ -81,6 +81,7 @@
     states_ref,
     after_ref,
     suffix_ref,
+    sent_ref,
     local_ref,
     grad_ref,
     total_ref,
@@ -120,15 +121,21 @@
             dyi = (dyt_ref[rows, :].astype(F32) * inflow_s[head, :]).astype(BF16)
             state = dot(xw, b_part)
             grad = dot(dyi, c_part)
-            states_ref[rows, :] = state
+            states_ref[rows, :] = state.astype(BF16)
             after = grad_ref[rows, :]
-            after_ref[rows, :] = after
+            after_ref[rows, :] = after.astype(BF16)
             local_ref[rows, :] += total_ref[head, :] * state
             grad_ref[rows, :] = decay_s[head, :] * after + grad
         return 0
 
-    lax.fori_loop(0, heads // 2, pair, 0)
+    lax.fori_loop(0, heads // 2, pair, 0, unroll=4)
     total_ref[...] = total_ref[...] * decay_s[...]
+
+    @pl.when(block == 0)
+    def _():
+        width = heads * head_dim
+        sent_ref[:width, :] = jnp.where(base_ref[0, 1] == 1, local_ref[...], grad_ref[...])
+        sent_ref[width:, :] = total_ref[...]
 
 
 def first_pass(doc, base, x, dy, maps, logits, head_params):
@@ -158,27 +165,26 @@
             per_block(width, state_n),
             per_block(width, state_n),
             per_block(heads, state_n),
-            whole(width, state_n),
-            whole(width, state_n),
-            whole(heads, state_n),
+            whole(width + heads, state_n),
         ],
         out_shape=[
             jax.ShapeDtypeStruct((groups, width, GROUP), BF16),
             jax.ShapeDtypeStruct((groups, width, GROUP), BF16),
-            jax.ShapeDtypeStruct((groups, width, state_n), F32),
-            jax.ShapeDtypeStruct((groups, width, state_n), F32),
+            jax.ShapeDtypeStruct((groups, width, state_n), BF16),
+            jax.ShapeDtypeStruct((groups, width, state_n), BF16),
             jax.ShapeDtypeStruct((groups, heads, state_n), F32),
-            jax.ShapeDtypeStruct((width, state_n), F32),
-            jax.ShapeDtypeStruct((width, state_n), F32),
-            jax.ShapeDtypeStruct((heads, state_n), F32),
+            jax.ShapeDtypeStruct((width + heads, state_n), F32),
         ],
         scratch_shapes=[
-            pltpu.VMEM((heads, GROUP), F32),
-            pltpu.VMEM((heads, GROUP), F32),
+            pltpu.VMEM((width, state_n), F32),
+            pltpu.VMEM((width, state_n), F32),
             pltpu.VMEM((heads, state_n), F32),
+            pltpu.VMEM((heads, GROUP), F32),
+            pltpu.VMEM((heads, GROUP), F32),
+            pltpu.VMEM((heads, state_n), F32),
         ],
         compiler_params=pltpu.CompilerParams(
-            dimension_semantics=("arbitrary",), vmem_limit_bytes=48 << 20
+            dimension_semantics=("arbitrary",), vmem_limit_bytes=63 << 20
         ),
         cost_estimate=pl.CostEstimate(
             flops=4 * length * width * state_n,
@@ -204,13 +210,14 @@
     states_ref,
     after_ref,
     suffix_ref,
-    entry_ref,
     exit_ref,
-    y_ref,
+    yt_ref,
     dx_ref,
     dmaps_ref,
     dlogits_ref,
     sums_ref,
+    rows_ref,
+    prefix_s,
     start_s,
     weight_s,
     inflow_s,
@@ -226,6 +233,7 @@
     dyi_s,
     out_s,
     in_s,
+    given_s,
     skip_s,
     ends_s,
 ):
@@ -236,7 +244,8 @@
 
     @pl.when(block == 0)
     def _():
-        start_s[...] = entry_ref[...]
+        start_s[...] = jnp.zeros_like(start_s)
+        prefix_s[...] = jnp.ones_like(prefix_s)
         sums_ref[...] = jnp.zeros_like(sums_ref)
         mix_s[...] = jnp.zeros_like(mix_s)
 
@@ -247,6 +256,9 @@
     weight_s[...] = weight
     inflow_s[...] = inflow
     decay_s[...] = jnp.broadcast_to(decay, decay_s.shape)
+    rows_ref[0] = inflow * prefix_s[:, 0:1]
+    prefix_s[...] = prefix_s[...] * decay
+    last = base_ref[0, 1].astype(F32)
     over = cum * LOG2E
     over_s[...] = over
     under = over - jnp.log2(step)
@@ -279,16 +291,38 @@
             head = pl.ds(h, 1)
             rows = pl.ds(pl.multiple_of(h * head_dim, head_dim), head_dim)
             lo = one * head_dim
-            after = suffix_ref[head, :] * exit_ref[rows, :] + after_ref[rows, :]
+            after = (suffix_ref[head, :] * last) * exit_ref[rows, :] + after_ref[rows, :].astype(F32)
             pair_suffix.append(after)
-            new = decay_s[head, :] * start[lo : lo + head_dim, :] + states_ref[rows, :]
+            new = decay_s[head, :] * start[lo : lo + head_dim, :] + states_ref[rows, :].astype(F32)
             next_parts.append(new)
-            ends_s[head, :] = jnp.sum(new * after, axis=0, keepdims=True)
+            ends_s[head, :] = jnp.sum(start[lo : lo + head_dim, :] * after, axis=0, keepdims=True)
         start_s[cols, :] = jnp.concatenate(next_parts, axis=0)
         after_b = jnp.concatenate(pair_suffix, axis=0).astype(BF16)
         after_t[:, cols] = after_b.T
         given = dot(after_b, b_t)
         x_pair = x_ref[:, cols]
+        wides = []
+        for one in range(2):
+            dyt = dyt_ref[pl.ds(pl.multiple_of(k * 2 * head_dim + one * head_dim, head_dim), head_dim), :]
+            zero = jnp.zeros_like(dyt)
+            wides.append(jnp.concatenate([dyt, zero] if one == 0 else [zero, dyt], axis=0))
+        for lo_j, lo_i in ((0, 0), (half, half)):
+            js = pl.ds(lo_j, half)
+            for at in range(lo_i, GROUP, half):
+                ins = pl.ds(at, half)
+                scores = scores_s[js, ins]
+                total = dscores_s[js, ins]
+                wide = jnp.concatenate([wide[:, at : at + half] for wide in wides], axis=1)
+                dmix = dot(x_pair[lo_j : lo_j + half, :], wide)
+                for one in range(2):
+                    h = k * 2 + one
+                    gap = over_s[pl.ds(h, 1), ins] - under_s[h, js, :]
+                    if at == lo_j:
+                        gap = jnp.minimum(gap, 64.0)
+                    shape = jnp.exp2(gap)
+                    mix_s[2 * k + one, js, ins] = (scores * shape).astype(BF16)
+                    total += dmix[:, one * half : (one + 1) * half] * shape
+                dscores_s[js, ins] = total
         for one in range(2):
             h = k * 2 + one
             head = pl.ds(h, 1)
@@ -296,21 +330,7 @@
             lo = one * head_dim
             xt = xt_ref[rows, :]
             dyt = dyt_ref[rows, :]
-            zero = jnp.zeros_like(dyt)
-            dyt_wide = jnp.concatenate([dyt, zero] if one == 0 else [zero, dyt], axis=0)
-            over_h = over_s[head, :]
-            for lo_j, lo_i in ((0, 0), (half, half)):
-                js = pl.ds(lo_j, half)
-                dmix = dot(x_pair[lo_j : lo_j + half, :], dyt_wide[:, lo_i:])
-                for at in range(lo_i, GROUP, half):
-                    ins = pl.ds(at, half)
-                    gap = over_h[:, at : at + half] - under_s[h, js, :]
-                    if at == lo_j:
-                        gap = jnp.minimum(gap, 64.0)
-                    shape = jnp.exp2(gap)
-                    mix_s[one, js, ins] = (scores_s[js, ins] * shape).astype(BF16)
-                    dscores_s[js, ins] += dmix[:, at - lo_i : at - lo_i + half] * shape
-            mix = mix_s[one]
+            mix = mix_s[h]
             x32 = xt.astype(F32)
             dy32 = dyt.astype(F32)
             skip = skip_ref[h]
@@ -322,39 +342,46 @@
             out_s[head, :] = jnp.sum(dy32 * y, axis=0, keepdims=True)
             skip_s[head, :] = jnp.sum(dy32 * x32, axis=0, keepdims=True)
             y_t = (y + skip * x32).astype(BF16)
-            dx = dot(dyt, mix, NT) + given[lo : lo + head_dim, :] * weight_h
+            dx = dot(dyt, mix, NT)
             in_s[head, :] = jnp.sum(x32 * dx, axis=0, keepdims=True)
-            dx_t = (dx + skip * dy32).astype(BF16)
+            from_state = given[lo : lo + head_dim, :] * weight_h
+            given_s[head, :] = jnp.sum(x32 * from_state, axis=0, keepdims=True)
+            dx_t = (dx + from_state + skip * dy32).astype(BF16)
+            yt_ref[rows, :] = y_t
             if one == 0:
-                kept = (y_t, dx_t)
+                kept = dx_t
             else:
-                y_ref[:, cols] = jnp.concatenate([kept[0], y_t], axis=0).T
-                dx_ref[:, cols] = jnp.concatenate([kept[1], dx_t], axis=0).T
+                dx_ref[:, cols] = jnp.concatenate([kept, dx_t], axis=0).T
         return 0
 
-    lax.fori_loop(0, heads // 2, pair, 0)
+    for k in range(heads // 2):
+        pair(k, 0)
 
     dscores = jnp.where(visible, dscores_s[...], 0.0).astype(BF16)
     dc_t = dot(start_t[...], dyi_s[...]) + dot(b_t, dscores)
     db_t = dot(after_t[...], xw_s[...]) + dot(c_t, dscores, NT)
-    dmaps_ref[:, :state_n] = db_t.T.astype(BF16)
-    dmaps_ref[:, state_n:] = dc_t.T.astype(BF16)
+    dmaps_ref[:state_n, :] = db_t
+    dmaps_ref[state_n:, :] = dc_t
 
     lane = lax.broadcasted_iota(jnp.int32, (heads, GROUP), 1)
-    ends = jnp.sum(ends_s[...], axis=1, keepdims=True)
+    ends = decay * jnp.sum(ends_s[...], axis=1, keepdims=True)
     inner = in_s[...]
-    dcum = out_s[...] - inner + jnp.where(lane == GROUP - 1, ends, 0.0)
-    dlog = running_sum(dcum, reverse=True)
-    dstep = inner / step - rate * dlog
-    dlogits = dstep * jax.nn.sigmoid(shifted)
+    given_sum = given_s[...]
+    before = jnp.where(lane > 0, pltpu.roll(running_sum(given_sum), 1, 1), 0.0)
+    dlog = running_sum(out_s[...] - inner, reverse=True) + before + ends
+    dstep = (inner + given_sum) / step - rate * dlog
+    slope = jax.nn.sigmoid(shifted)
+    dlogits = dstep * slope
     dlogits_ref[...] = dlogits
+    rows_ref[1] = rate * slope
+    rows_ref[2] = step * rate
     sums_ref[0] += -step * rate * dlog
     sums_ref[1] += dlogits
     sums_ref[2] += skip_s[...]
 
 
 def second_pass(
-    doc, base, skip_gain, x, xt, dyt, maps, logits, head_params, states, after, suffix, entry, leave
+    doc, base, skip_gain, x, xt, dyt, maps, logits, head_params, states, after, suffix, received
 ):
     length, width = x.shape
     heads = logits.shape[0]
@@ -380,24 +407,26 @@
             per_block(width, state_n),
             per_block(width, state_n),
             per_block(heads, state_n),
-            whole(width, state_n),
-            whole(width, state_n),
+            whole(width + heads, state_n),
         ],
         out_specs=[
+            per_block(width, GROUP),
             pl.BlockSpec((GROUP, width), lambda i: (i, 0)),
-            pl.BlockSpec((GROUP, width), lambda i: (i, 0)),
-            pl.BlockSpec((GROUP, 2 * state_n), lambda i: (i, 0)),
-            pl.BlockSpec((heads, GROUP), lambda i: (0, i)),
+            per_block(2 * state_n, GROUP),
+            per_block(heads, GROUP),
             pl.BlockSpec((3, heads, GROUP), lambda i: (0, 0, 0)),
+            pl.BlockSpec((None, 3, heads, GROUP), lambda i: (i, 0, 0, 0)),
         ],
         out_shape=[
+            jax.ShapeDtypeStruct((groups, width, GROUP), BF16),
             jax.ShapeDtypeStruct((length, width), BF16),
-            jax.ShapeDtypeStruct((length, width), BF16),
-            jax.ShapeDtypeStruct((length, 2 * state_n), BF16),
-            jax.ShapeDtypeStruct((heads, length), F32),
+            jax.ShapeDtypeStruct((groups, 2 * state_n, GROUP), F32),
+            jax.ShapeDtypeStruct((groups, heads, GROUP), F32),
             jax.ShapeDtypeStruct((3, heads, GROUP), F32),
+            jax.ShapeDtypeStruct((groups, 3, heads, GROUP), F32),
         ],
         scratch_shapes=[
+            pltpu.VMEM((heads, state_n), F32),
             pltpu.VMEM((width, state_n), F32),
             pltpu.VMEM((heads, GROUP), F32),
             pltpu.VMEM((heads, GROUP), F32),
@@ -406,7 +435,7 @@
             pltpu.VMEM((heads, GROUP, half), F32),
             pltpu.VMEM((GROUP, GROUP), F32),
             pltpu.VMEM((GROUP, GROUP), F32),
-            pltpu.VMEM((2, GROUP, GROUP), BF16),
+            pltpu.VMEM((heads, GROUP, GROUP), BF16),
             pltpu.VMEM((state_n, width), BF16),
             pltpu.VMEM((state_n, width), BF16),
             pltpu.VMEM((width, GROUP), BF16),
@@ -414,10 +443,11 @@
             pltpu.VMEM((heads, GROUP), F32),
             pltpu.VMEM((heads, GROUP), F32),
             pltpu.VMEM((heads, GROUP), F32),
+            pltpu.VMEM((heads, GROUP), F32),
             pltpu.VMEM((heads, state_n), F32),
         ],
         compiler_params=pltpu.CompilerParams(
-            dimension_semantics=("arbitrary",), vmem_limit_bytes=56 << 20
+            dimension_semantics=("arbitrary",), vmem_limit_bytes=63 << 20
         ),
         cost_estimate=pl.CostEstimate(
             flops=groups * heads * GROUP * (6 * GROUP * 64 + 8 * 64 * state_n),
@@ -425,15 +455,189 @@
             transcendentals=heads * length * GROUP,
         ),
         name="second_pass",
-    )(doc, base, skip_gain, x, xt, dyt, maps, logits, head_params, states, after, suffix, entry, leave)
-
-
-def sent_to_successor(block, owner):
-    streams = lax.axis_size("stream")
-    pieces = block.reshape(streams, -1)
-    dealt = lax.all_to_all(pieces, "stream", 0, 0, tiled=True)
-    chosen = jnp.take(dealt, owner, axis=0)
-    return lax.all_to_all(chosen, "stream", 0, 0, tiled=True).reshape(block.shape)
+    )(doc, base, skip_gain, x, xt, dyt, maps, logits, head_params, states, after, suffix, received)
+
+
+def third_kernel(
+    heads,
+    head_dim,
+    base_ref,
+    dyt_ref,
+    maps_ref,
+    dlogits_in,
+    sums_in,
+    rows_ref,
+    own_ref,
+    other_ref,
+    received_ref,
+    total_ref,
+    dlogits_ref,
+    sums_ref,
+    entry_ref,
+    later_s,
+    brought_s,
+    totals_s,
+):
+    step_id = pl.program_id(0)
+    state_n = maps_ref.shape[1] // 2
+    width = heads * head_dim
+    mid = width // 2
+    is_first = base_ref[0, 1] == 1
+
+    @pl.when(step_id == 0)
+    def _():
+        totals_s[...] = sums_in[...]
+        for h in range(heads):
+            rows = slice(h * head_dim, (h + 1) * head_dim)
+            here = slice(h * head_dim % mid, h * head_dim % mid + head_dim)
+            low = h * head_dim < mid
+            start = jnp.where(is_first == low, own_ref[here, :], other_ref[here, :])
+            carried = received_ref[width + h : width + h + 1, :] * start + received_ref[rows, :]
+            entry = jnp.where(is_first, start, carried)
+            entry_ref[rows, :] = entry.astype(BF16)
+            through = total_ref[h : h + 1, :] * entry
+            meets = jnp.where(is_first, received_ref[rows, :], 0.0)
+            later_s[h : h + 1, :] = jnp.sum(through * meets, axis=0, keepdims=True)
+        later_s[...] = jnp.broadcast_to(jnp.sum(later_s[...], axis=1, keepdims=True), later_s.shape)
+
+    c_t = maps_ref[:, state_n:].T
+    for k in range(heads // 2):
+        lo = k * 2 * head_dim
+        carried = dot(entry_ref[lo : lo + 2 * head_dim, :], c_t)
+        for one in range(2):
+            h = 2 * k + one
+            rows = slice(h * head_dim, (h + 1) * head_dim)
+            meeting = dyt_ref[rows, :].astype(F32) * carried[one * head_dim : (one + 1) * head_dim, :]
+            brought_s[h : h + 1, :] = jnp.sum(meeting, axis=0, keepdims=True)
+    brought = brought_s[...] * rows_ref[0]
+    later = later_s[:, 0:1]
+    dlog = running_sum(brought, reverse=True) + later
+    later_s[...] = later_s[...] + jnp.sum(brought, axis=1, keepdims=True)
+    dlogits = rows_ref[1] * dlog
+    dlogits_ref[...] = dlogits_in[...] - dlogits
+    totals_s[0] -= rows_ref[2] * dlog
+    totals_s[1] -= dlogits
+
+    @pl.when(step_id == pl.num_programs(0) - 1)
+    def _():
+        sums_ref[...] = jnp.sum(totals_s[...], axis=2)
+
+
+def third_pass(base, dyt, maps, dlogits, sums, rows, own, other, received, sent):
+    groups, width, _ = dyt.shape
+    heads = rows.shape[2]
+    length = groups * GROUP
+    state_n = maps.shape[1] // 2
+    back = lambda i: groups - 1 - i
+    smem = pl.BlockSpec(memory_space=pltpu.SMEM)
+    per_block = lambda rows, cols: pl.BlockSpec((None, rows, cols), lambda i: (back(i), 0, 0))
+    whole = lambda rows, cols: pl.BlockSpec((rows, cols), lambda i: (0, 0))
+    return pl.pallas_call(
+        functools.partial(third_kernel, heads, width // heads),
+        grid=(groups,),
+        in_specs=[
+            smem,
+            per_block(width, GROUP),
+            pl.BlockSpec((GROUP, 2 * state_n), lambda i: (back(i), 0)),
+            per_block(heads, GROUP),
+            pl.BlockSpec((3, heads, GROUP), lambda i: (0, 0, 0)),
+            pl.BlockSpec((None, 3, heads, GROUP), lambda i: (back(i), 0, 0, 0)),
+            whole(width // 2, state_n),
+            whole(width // 2, state_n),
+            whole(width + heads, state_n),
+            pl.BlockSpec((heads, state_n), lambda i: (width // heads, 0)),
+        ],
+        out_specs=[
+            pl.BlockSpec((heads, GROUP), lambda i: (0, back(i))),
+            whole(3, heads),
+            whole(width, state_n),
+        ],
+        out_shape=[
+            jax.ShapeDtypeStruct((heads, length), F32),
+            jax.ShapeDtypeStruct((3, heads), F32),
+            jax.ShapeDtypeStruct((width, state_n), BF16),
+        ],
+        scratch_shapes=[
+            pltpu.VMEM((heads, state_n), F32),
+            pltpu.VMEM((heads, GROUP), F32),
+            pltpu.VMEM((3, heads, GROUP), F32),
+        ],
+        compiler_params=pltpu.CompilerParams(
+            dimension_semantics=("arbitrary",), vmem_limit_bytes=63 << 20
+        ),
+        cost_estimate=pl.CostEstimate(
+            flops=2 * length * width * state_n, bytes_accessed=2 * length * width, transcendentals=0
+        ),
+        name="third_pass",
+    )(base, dyt, maps, dlogits, sums, rows, own, other, received, sent)
+
+
+def fourth_kernel(
+    heads, head_dim, yt_ref, dyt_ref, maps_ref, dmaps_in, rows_ref, entry_ref, y_ref, dmaps_ref, entry_t, dyi_s
+):
+    state_n = maps_ref.shape[1] // 2
+    width = heads * head_dim
+
+    @pl.when(pl.program_id(0) == 0)
+    def _():
+        for at in range(0, width, state_n):
+            entry_t[:, at : at + state_n] = entry_ref[at : at + state_n, :].T
+
+    c_t = maps_ref[:, state_n:].T
+    for k in range(heads // 2):
+        lo = k * 2 * head_dim
+        carried = dot(entry_ref[lo : lo + 2 * head_dim, :], c_t)
+        ys = []
+        for one in range(2):
+            h = 2 * k + one
+            rows = slice(h * head_dim, (h + 1) * head_dim)
+            reach = rows_ref[0, h : h + 1, :]
+            dyi_s[rows, :] = (dyt_ref[rows, :].astype(F32) * reach).astype(BF16)
+            brought = carried[one * head_dim : (one + 1) * head_dim, :] * reach
+            ys.append((yt_ref[rows, :].astype(F32) + brought).astype(BF16))
+        y_ref[:, lo : lo + 2 * head_dim] = jnp.concatenate(ys, axis=0).T
+    dc_t = dmaps_in[state_n:, :] + dot(entry_t[...], dyi_s[...])
+    dmaps_ref[:, :state_n] = dmaps_in[:state_n, :].T.astype(BF16)
+    dmaps_ref[:, state_n:] = dc_t.T.astype(BF16)
+
+
+def fourth_pass(yt, dyt, maps, dmaps, rows, entry):
+    groups, width, _ = yt.shape
+    heads = rows.shape[2]
+    length = groups * GROUP
+    state_n = maps.shape[1] // 2
+    per_block = lambda rows, cols: pl.BlockSpec((None, rows, cols), lambda i: (i, 0, 0))
+    return pl.pallas_call(
+        functools.partial(fourth_kernel, heads, width // heads),
+        grid=(groups,),
+        in_specs=[
+            per_block(width, GROUP),
+            per_block(width, GROUP),
+            pl.BlockSpec((GROUP, 2 * state_n), lambda i: (i, 0)),
+            per_block(2 * state_n, GROUP),
+            pl.BlockSpec((None, 1, heads, GROUP), lambda i: (i, 0, 0, 0)),
+            pl.BlockSpec((width, state_n), lambda i: (0, 0)),
+        ],
+        out_specs=[
+            pl.BlockSpec((GROUP, width), lambda i: (i, 0)),
+            pl.BlockSpec((GROUP, 2 * state_n), lambda i: (i, 0)),
+        ],
+        out_shape=[
+            jax.ShapeDtypeStruct((length, width), BF16),
+            jax.ShapeDtypeStruct((length, 2 * state_n), BF16),
+        ],
+        scratch_shapes=[
+            pltpu.VMEM((state_n, width), BF16),
+            pltpu.VMEM((width, GROUP), BF16),
+        ],
+        compiler_params=pltpu.CompilerParams(
+            dimension_semantics=("arbitrary",), vmem_limit_bytes=63 << 20
+        ),
+        cost_estimate=pl.CostEstimate(
+            flops=4 * length * width * state_n, bytes_accessed=6 * length * width, transcendentals=0
+        ),
+        name="fourth_pass",
+    )(yt, dyt, maps, dmaps, rows, entry)
 
 
 def shards(
@@ -451,39 +655,37 @@
     length, width = head_inputs.shape[1:]
     heads = step_logits.shape[1]
     state_n = old_states.shape[3]
-    head_dim = old_states.shape[2]
     seq_index = lax.axis_index("seq")
-    is_first = seq_index == 0
+    streams = lax.axis_size("stream")
     swap = [(0, 1), (1, 0)]
-    base = (seq_index * length).astype(jnp.int32).reshape(1, 1)
+    base = jnp.stack([seq_index * length, 1 - seq_index]).astype(jnp.int32).reshape(1, 2)
     head_params = jnp.stack([log_rates, step_bias], axis=1)
-
-    own = sent_to_successor(old_states[0], old_owner).reshape(width // 2, state_n)
-
     x, dy, maps, logits = head_inputs[0], grad_output[0], state_maps[0], step_logits[0]
-    xt, dyt, states, after, suffix, local, grad, total = first_pass(
+
+    dealt = lax.all_to_all(old_states[0].reshape(streams, -1), "stream", 0, 0, tiled=True)
+    xt, dyt, states, after, suffix, sent = first_pass(
         doc_starts, base, x, dy, maps, logits, head_params
     )
+    dealt, sent = lax.optimization_barrier((dealt, sent))
+    received = lax.ppermute(sent, "seq", swap)
+    dealt, received = lax.optimization_barrier((dealt, received))
+    own = lax.all_to_all(
+        dealt.at[old_owner].get(mode="promise_in_bounds"), "stream", 0, 0, tiled=True)
+    yt, dx, dmaps, dlogits, sums, rows = second_pass(
+        doc_starts, base, skip_gain, x, xt, dyt, maps, logits, head_params,
+        states, after, suffix, received,
+    )
+    own, sums = lax.optimization_barrier((own, sums))
+    own = own.reshape(width // 2, state_n)
     other = lax.ppermute(own, "seq", swap)
-    start = jnp.where(
-        is_first, jnp.concatenate([own, other], axis=0), jnp.concatenate([other, own], axis=0)
+    dlogits, sums, entry = third_pass(
+        base, dyt, maps, dlogits, sums, rows, own, other, received, sent
     )
-    scaled = (total[:, None, :] * start.reshape(heads, head_dim, state_n)).reshape(width, state_n)
-    sent = jnp.where(is_first, scaled + local, grad)
-    received = lax.ppermute(sent, "seq", swap)
-    entry = jnp.where(is_first, start, received)
-    leave = jnp.where(is_first, received, 0.0)
-    y, dx, dmaps, dlogits, sums = second_pass(
-        doc_starts, base, skip_gain, x, xt, dyt, maps, logits, head_params,
-        states, after, suffix, entry, leave,
-    )
-    totals = jnp.sum(sums, axis=2)
-    totals = totals + lax.ppermute(totals, "seq", swap)
-    streams = lax.axis_size("stream")
-    by = 1
-    while by < streams:
-        totals = totals + lax.ppermute(totals, "stream", [(s, s ^ by) for s in range(streams)])
-        by *= 2
+    devices = streams * lax.axis_size("seq")
+    everyone = jnp.broadcast_to(sums.reshape(1, -1), (devices, sums.size))
+    gathered = lax.all_to_all(everyone, ("stream", "seq"), 0, 0, tiled=True)
+    y, dmaps = fourth_pass(yt, dyt, maps, dmaps, rows, entry)
+    totals = jnp.sum(gathered, axis=0).reshape(sums.shape)
     return (y[None], dx[None], dmaps[None], dlogits[None], totals[0], totals[1], totals[2])
 
 

time: 149 us -> 112 us (0.75)
  waiting for transfers between devices: 35.3 us -> 4.31 us
  blocking collectives: 15.9 us -> 0 us
  starting transfers between devices: 16.7 us -> 32 us
  Pallas kernels: 74.3 us -> 67.5 us
  local copies, waits for them, and re-layouts: 2.12 us -> 5.37 us
  other arithmetic: 3.99 us -> 1.43 us
    ppermute x7 -> x0, waiting for transfers between devices: 22.7 us -> none  [the longest x6 21.9 us: shards(): lax.ppermute(totals, 'stream', [(s, s ^ by) for s in range(streams)])]
    all_to_all x1 -> x3, starting transfers between devices: 11.6 us -> 31.8 us  [the longest x1 11.5 us: shards(): lax.all_to_all(old_states[0].reshape(streams, -1), 'stream', 0, 0, tiled=...]
    pallas_call x0 -> x2, Pallas kernels: none -> 19 us  [the longest x1 9.76 us: fourth_pass(): pl.pallas_call(functools.partial(fourth_kernel, heads, width // heads), g...]
    pallas_call x1, Pallas kernels: 49.7 us -> 33.2 us  [second_pass(): pl.pallas_call(functools.partial(second_kernel, heads, width // heads), g...]
    all_to_all x1 -> x0, blocking collectives: 15.9 us -> none  [sent_to_successor(): lax.all_to_all(chosen, 'stream', 0, 0, tiled=True).reshape(block.shape)]
    all_to_all x1 -> x3, waiting for transfers between devices: 10.6 us -> 0.01 us  [the longest x1 0.01 us: shards(): lax.all_to_all(old_states[0].reshape(streams, -1), 'stream', 0, 0, tiled=...]
    pallas_call x1, Pallas kernels: 24.6 us -> 15.3 us  [first_pass(): pl.pallas_call(functools.partial(first_kernel, heads, width // heads), gr...]
    ppermute x7 -> x0, starting transfers between devices: 4.55 us -> none  [the longest x6 4.09 us: shards(): lax.ppermute(totals, 'stream', [(s, s ^ by) for s in range(streams)])]
  transfers between devices with their start and end apart: 10 -> 5, of which waited for: 9 -> 2; matrix products, arithmetic and copies ran while one was open for 1% -> 2% of each run, Pallas kernels for 16% -> 52%
where the time goes in v2:
time: 112 us; the launch traced here: 111 us
  Pallas kernels  67.5 us (60%)
  starting transfers between devices  32 us (29%)
  local copies, waits for them, and re-layouts  5.37 us (5%)
  waiting for transfers between devices  4.31 us (4%)
  other arithmetic  1.43 us (1%)
    pallas_call x1, Pallas kernels, second_pass(): pl.pallas_call(functools.partial(second_kernel, heads, width // heads), g...  33.2 us
    pallas_call x1, Pallas kernels, first_pass(): pl.pallas_call(functools.partial(first_kernel, heads, width // heads), gr...  15.3 us
    all_to_all x1, starting transfers between devices, shards(): lax.all_to_all(old_states[0].reshape(streams, -1), 'stream', 0, 0, tiled=...  11.5 us
    all_to_all x1, starting transfers between devices, shards(): lax.all_to_all(dealt.at[old_owner].get(mode='promise_in_bounds'), 'stream...  10.3 us
    all_to_all x1, starting transfers between devices, shards(): gathered = lax.all_to_all(everyone, ('stream', 'seq'), 0, 0, tiled=True)  9.98 us
    pallas_call x1, Pallas kernels, fourth_pass(): pl.pallas_call(functools.partial(fourth_kernel, heads, width // heads), g...  9.76 us
    pallas_call x1, Pallas kernels, third_pass(): pl.pallas_call(functools.partial(third_kernel, heads, width // heads), gr...  9.21 us
    ppermute x1, waiting for transfers between devices, shards(): received = lax.ppermute(sent, 'seq', swap)  2.6 us
  transfers between devices with their start and end apart: 5, of which 2 were waited for; matrix products, arithmetic and copies ran while one was open for 2% of the time, Pallas kernels for 52%

profile of v2, /device:TPU:0, one launch (start us, length us, event | category | flops | bytes accessed | tf_op | source)
XLA Modules:
  0.0 111.4 jit_solution(16109317973394185796)
XLA Ops:
  0.6 11.5 %all-to-all-start = ((f32[64,1,1536]{2,1,0:T(1,128)}), f32[64,1,1536]{2,1,0:T(1,128)S(1)}, u32[]{:S(2)}, u32[]{:S(2)}) async-start(f32[64,1,1536]{2,1,0:T(1,128)} %bitcast.32), calls=%async_computation | async-start | bytes 786432 | tf_op jit(solution)/shard_map/all_to_all | solution.py:665
  12.2 0.7 pad_maximum_fusion
  12.8 0.7 copy.25.heads_ref
  13.5 0.6 add_bitcast_fusion.base_ref
  14.1 0.0 copy-start.2
  14.1 15.3 %first_pass.1 = (bf16[6,1536,256]{2,1,0:T(8,128)(2,1)}, bf16[6,1536,256]{2,1,0:T(8,128)(2,1)}, bf16[6,1536,128]{2,1,0:T(8,128)(2,1)}, bf16[6,1536,128]{2,1,0:T(8...) custom-call(s32[1,2]{1,0:T(1,128)} %doc_ref.3, s32[1,2]{1,0:T(1,128)} %add_bitcast_fusion.base_ref, ...), custom_call_target="tpu_custom_call" | custom-call | flops 1207959552 | bytes 28311552 | tf_op jit(solution)/shard_map/first_pass/pallas_call | solution.py:150
  29.4 0.0 all-to-all-done
  29.5 0.1 collective-permute-start
  29.6 0.0 copy-done.2
  29.6 2.6 %collective-permute-done.exit_ref.received_ref = f32[1560,128]{1,0:T(8,128)} collective-permute-done((f32[1560,128]{1,0:T(8,128)}, f32[1560,128]{1,0:T(8,128)}, u32[]{:S(2)}, u32[]{:S(2)}) %collective-permute-start) | collective-permute-done | bytes 798752 | tf_op jit(solution)/shard_map/ppermute | solution.py:670
  32.2 0.7 gather_fusion
  32.9 1.2 %copy.27 = f32[64,1,1536]{2,1,0:T(1,128)} copy(f32[64,1,1536]{2,0,1:T(8,128)S(1)} %bitcast.31) | data formatting | bytes 786432 | tf_op jit(solution)/shard_map/all_to_all | solution.py:672
  34.1 10.3 %all-to-all-start.1 = ((f32[64,1,1536]{2,1,0:T(1,128)}), f32[64,1,1536]{2,1,0:T(1,128)S(1)}, u32[]{:S(2)}, u32[]{:S(2)}) async-start(f32[64,1,1536]{2,1,0:T(1,128)} %copy.27), calls=%async_computation.1 | async-start | bytes 786432 | tf_op jit(solution)/shard_map/all_to_all | solution.py:672
  44.4 33.2 %second_pass.1 = (bf16[6,1536,256]{2,1,0:T(8,128)(2,1)}, bf16[1536,1536]{1,0:T(8,128)(2,1)}, f32[6,256,256]{2,1,0:T(8,128)}, f32[6,24,256]{2,1,0:T(8,128)}, f32[...) custom-call(s32[1,2]{1,0:T(1,128)} %doc_ref.3, s32[1,2]{1,0:T(1,128)} %add_bitcast_fusion.base_ref, f32[24]{0:T(128)} %skip_ref.1, ...), custom_call_target="tpu_custom_call" | custom-call | flops 6039797760 | bytes 33030144 | tf_op jit(solution)/shard_map/second_pass/pallas_call | solution.py:394
  77.6 0.0 all-to-all-done.1
  77.7 0.0 copy-start
  77.7 0.1 collective-permute-start.1
  77.8 1.7 %collective-permute-done.1.other_ref = f32[768,128]{1,0:T(8,128)S(1)} collective-permute-done((f32[768,128]{1,0:T(8,128)S(1)}, f32[768,128]{1,0:T(8,128)S(1)}, u32[]{:S(2)}, u32[]{:S(2)}) %collective-permute-start.1) | collective-permute-done | bytes 393248 | tf_op jit(solution)/shard_map/ppermute | solution.py:680
  79.5 0.0 copy-start.1
  79.5 0.0 copy-done
  79.5 0.7 copy-done.1
  80.3 9.2 %third_pass.1 = (f32[24,1536]{1,0:T(8,128)}, f32[3,24]{1,0:T(4,128)}, bf16[1536,128]{1,0:T(8,128)(2,1)}) custom-call(s32[1,2]{1,0:T(1,128)} %add_bitcast_fusion.base_ref, bf16[6,1536,256]{2,1,0:T(8,128)(2,1)} %get-tuple-element.31.dyt_ref, bf16[1536,256]{1,0:T(8,128)(2,1)} %bitcast.25, f32[6,24,256]{2,1,0:T(8,128)} %get-tuple-element.42.dlogits_in, ...), custom_call_target="tpu_custom_call" | custom-call | flops 603979776 | bytes 4718592 | tf_op jit(solution)/shard_map/third_pass/pallas_call | solution.py:535
  89.5 0.7 broadcast_in_dim.27
  90.2 0.7 broadcast_in_dim.28
  90.9 10.0 %all-to-all-start.2 = ((f32[128,1,72]{2,1,0:T(1,128)}), f32[128,1,72]{2,1,0:T(1,128)S(1)}, u32[]{:S(2)}, u32[]{:S(2)}) async-start(f32[128,1,72]{2,1,0:T(1,128)} %broadcast_in_dim.28), calls=%async_computation.2 | async-start | bytes 131072 | tf_op jit(solution)/shard_map/all_to_all | solution.py:686
  100.9 9.8 %fourth_pass.1 = (bf16[1536,1536]{1,0:T(8,128)(2,1)}, bf16[1536,256]{1,0:T(8,128)(2,1)}) custom-call(bf16[6,1536,256]{2,1,0:T(8,128)(2,1)} %get-tuple-element.39.yt_ref, bf16[6,1536,256]{2,1,0:T(8,128)(2,1)} %get-tuple-element.31.dyt_ref, bf16[1536,256]{1,0:T(8,128)(2,1)} %bitcast.26, f32[6,256,256]{2,1,0:T(8,128)} %get-tuple-element.40.dmaps_in, ...), custom_call_target="tpu_custom_call" | custom-call | flops 1207959552 | bytes 14155776 | tf_op jit(solution)/shard_map/fourth_pass/pallas_call | solution.py:610
  110.6 0.0 all-to-all-done.2
  110.6 0.2 reduce_sum.9
  110.8 0.6 fusion
  (5 shorter events, 0.1 us)
Async XLA Ops:
  0.6 28.8 %all-to-all-start = ((f32[64,1,1536]{2,1,0:T(1,128)}), f32[64,1,1536]{2,1,0:T(1,128)S(1)}, u32[]{:S(2)}, u32[]{:S(2)}) async-start(f32[64,1,1536]{2,1,0:T(1,128)} %bitcast.32), calls=%async_computation | async-start | bytes 786432 | tf_op jit(solution)/shard_map/all_to_all | solution.py:665
  14.1 15.5 %copy-start.2 = (s32[64]{0:T(128)S(1)}, s32[64]{0:T(128)}, u32[]{:S(2)}) copy-start(s32[64]{0:T(128)} %param.17) | copy-start | bytes 772
  29.5 2.7 %collective-permute-start = (f32[1560,128]{1,0:T(8,128)}, f32[1560,128]{1,0:T(8,128)}, u32[]{:S(2)}, u32[]{:S(2)}) collective-permute-start(f32[1560,128]{1,0:T(8,128)} %get-tuple-element.37.total_ref), channel_id=1, source_target_pairs={{0,1},{1,0},{2,3},{3,2},{4,5},{5,4},{6,7},{7,6},{8,9},{9,8},{10,11... | collective-permute-start | bytes 2396168 | tf_op jit(solution)/shard_map/ppermute | solution.py:670
  34.1 43.6 %all-to-all-start.1 = ((f32[64,1,1536]{2,1,0:T(1,128)}), f32[64,1,1536]{2,1,0:T(1,128)S(1)}, u32[]{:S(2)}, u32[]{:S(2)}) async-start(f32[64,1,1536]{2,1,0:T(1,128)} %copy.27), calls=%async_computation.1 | async-start | bytes 786432 | tf_op jit(solution)/shard_map/all_to_all | solution.py:672
  77.7 1.8 %copy-start = (f32[768,128]{1,0:T(8,128)}, f32[768,128]{1,0:T(8,128)S(1)}, u32[]{:S(2)}) copy-start(f32[768,128]{1,0:T(8,128)S(1)} %reshape.42.own_ref) | copy-start | bytes 1179652
  77.7 1.8 %collective-permute-start.1 = (f32[768,128]{1,0:T(8,128)S(1)}, f32[768,128]{1,0:T(8,128)S(1)}, u32[]{:S(2)}, u32[]{:S(2)}) collective-permute-start(f32[768,128]{1,0:T(8,128)S(1)} %reshape.42.own_ref), channel_id=1, source_target_pairs={{0,1},{1,0},{2,3},{3,2},{4,5},{5,4},{6,7},{7,6},{8,9},{9,8},{10,11... | collective-permute-start | bytes 1179656 | tf_op jit(solution)/shard_map/ppermute | solution.py:680
  79.5 0.7 copy-start.1
  90.9 19.7 %all-to-all-start.2 = ((f32[128,1,72]{2,1,0:T(1,128)}), f32[128,1,72]{2,1,0:T(1,128)S(1)}, u32[]{:S(2)}, u32[]{:S(2)}) async-start(f32[128,1,72]{2,1,0:T(1,128)} %broadcast_in_dim.28), calls=%async_computation.2 | async-start | bytes 131072 | tf_op jit(solution)/shard_map/all_to_all | solution.py:686

commit v3 on v2

--- a/solution.py
+++ b/solution.py
@@ -8,6 +8,8 @@
 from jax.sharding import PartitionSpec as P
 
 GROUP = 256
+THIRD_BLOCKS = 6
+FOURTH_BLOCKS = 3
 LOG2E = 1.4426950408889634
 F32 = jnp.float32
 BF16 = jnp.bfloat16
@@ -76,12 +78,12 @@
     maps_ref,
     logits_ref,
     heads_ref,
-    xt_ref,
-    dyt_ref,
     states_ref,
     after_ref,
     suffix_ref,
     sent_ref,
+    xt_ref,
+    dyt_ref,
     local_ref,
     grad_ref,
     total_ref,
@@ -128,7 +130,7 @@
             grad_ref[rows, :] = decay_s[head, :] * after + grad
         return 0
 
-    lax.fori_loop(0, heads // 2, pair, 0, unroll=4)
+    lax.fori_loop(0, heads // 2, pair, 0, unroll=6)
     total_ref[...] = total_ref[...] * decay_s[...]
 
     @pl.when(block == 0)
@@ -160,22 +162,20 @@
             whole(heads, head_params.shape[1]),
         ],
         out_specs=[
-            per_block(width, GROUP),
-            per_block(width, GROUP),
             per_block(width, state_n),
             per_block(width, state_n),
             per_block(heads, state_n),
             whole(width + heads, state_n),
         ],
         out_shape=[
-            jax.ShapeDtypeStruct((groups, width, GROUP), BF16),
-            jax.ShapeDtypeStruct((groups, width, GROUP), BF16),
             jax.ShapeDtypeStruct((groups, width, state_n), BF16),
             jax.ShapeDtypeStruct((groups, width, state_n), BF16),
             jax.ShapeDtypeStruct((groups, heads, state_n), F32),
             jax.ShapeDtypeStruct((width + heads, state_n), F32),
         ],
         scratch_shapes=[
+            pltpu.VMEM((width, GROUP), BF16),
+            pltpu.VMEM((width, GROUP), BF16),
             pltpu.VMEM((width, state_n), F32),
             pltpu.VMEM((width, state_n), F32),
             pltpu.VMEM((heads, state_n), F32),
@@ -202,8 +202,7 @@
     base_ref,
     skip_ref,
     x_ref,
-    xt_ref,
-    dyt_ref,
+    dy_ref,
     maps_ref,
     logits_ref,
     heads_ref,
@@ -217,6 +216,8 @@
     dlogits_ref,
     sums_ref,
     rows_ref,
+    dyt_ref,
+    xt_ref,
     prefix_s,
     start_s,
     weight_s,
@@ -301,6 +302,8 @@
         after_t[:, cols] = after_b.T
         given = dot(after_b, b_t)
         x_pair = x_ref[:, cols]
+        xt_ref[cols, :] = x_pair.T
+        dyt_ref[cols, :] = dy_ref[:, cols].T
         wides = []
         for one in range(2):
             dyt = dyt_ref[pl.ds(pl.multiple_of(k * 2 * head_dim + one * head_dim, head_dim), head_dim), :]
@@ -381,7 +384,7 @@
 
 
 def second_pass(
-    doc, base, skip_gain, x, xt, dyt, maps, logits, head_params, states, after, suffix, received
+    doc, base, skip_gain, x, dy, maps, logits, head_params, states, after, suffix, received
 ):
     length, width = x.shape
     heads = logits.shape[0]
@@ -399,8 +402,7 @@
             smem,
             smem,
             pl.BlockSpec((GROUP, width), lambda i: (i, 0)),
-            per_block(width, GROUP),
-            per_block(width, GROUP),
+            pl.BlockSpec((GROUP, width), lambda i: (i, 0)),
             pl.BlockSpec((GROUP, 2 * state_n), lambda i: (i, 0)),
             pl.BlockSpec((heads, GROUP), lambda i: (0, i)),
             whole(heads, head_params.shape[1]),
@@ -416,6 +418,7 @@
             per_block(heads, GROUP),
             pl.BlockSpec((3, heads, GROUP), lambda i: (0, 0, 0)),
             pl.BlockSpec((None, 3, heads, GROUP), lambda i: (i, 0, 0, 0)),
+            per_block(width, GROUP),
         ],
         out_shape=[
             jax.ShapeDtypeStruct((groups, width, GROUP), BF16),
@@ -424,8 +427,10 @@
             jax.ShapeDtypeStruct((groups, heads, GROUP), F32),
             jax.ShapeDtypeStruct((3, heads, GROUP), F32),
             jax.ShapeDtypeStruct((groups, 3, heads, GROUP), F32),
+            jax.ShapeDtypeStruct((groups, width, GROUP), BF16),
         ],
         scratch_shapes=[
+            pltpu.VMEM((width, GROUP), BF16),
             pltpu.VMEM((heads, state_n), F32),
             pltpu.VMEM((width, state_n), F32),
             pltpu.VMEM((heads, GROUP), F32),
@@ -455,7 +460,7 @@
             transcendentals=heads * length * GROUP,
         ),
         name="second_pass",
-    )(doc, base, skip_gain, x, xt, dyt, maps, logits, head_params, states, after, suffix, received)
+    )(doc, base, skip_gain, x, dy, maps, logits, head_params, states, after, suffix, received)
 
 
 def third_kernel(
@@ -500,61 +505,70 @@
             later_s[h : h + 1, :] = jnp.sum(through * meets, axis=0, keepdims=True)
         later_s[...] = jnp.broadcast_to(jnp.sum(later_s[...], axis=1, keepdims=True), later_s.shape)
 
-    c_t = maps_ref[:, state_n:].T
-    for k in range(heads // 2):
-        lo = k * 2 * head_dim
-        carried = dot(entry_ref[lo : lo + 2 * head_dim, :], c_t)
-        for one in range(2):
-            h = 2 * k + one
-            rows = slice(h * head_dim, (h + 1) * head_dim)
-            meeting = dyt_ref[rows, :].astype(F32) * carried[one * head_dim : (one + 1) * head_dim, :]
-            brought_s[h : h + 1, :] = jnp.sum(meeting, axis=0, keepdims=True)
-    brought = brought_s[...] * rows_ref[0]
-    later = later_s[:, 0:1]
-    dlog = running_sum(brought, reverse=True) + later
-    later_s[...] = later_s[...] + jnp.sum(brought, axis=1, keepdims=True)
-    dlogits = rows_ref[1] * dlog
-    dlogits_ref[...] = dlogits_in[...] - dlogits
-    totals_s[0] -= rows_ref[2] * dlog
-    totals_s[1] -= dlogits
+    for part in reversed(range(dyt_ref.shape[0])):
+        here = slice(part * GROUP, (part + 1) * GROUP)
+        c_t = maps_ref[here, state_n:].T
+        for k in range(heads // 2):
+            lo = k * 2 * head_dim
+            carried = dot(entry_ref[lo : lo + 2 * head_dim, :], c_t)
+            for one in range(2):
+                h = 2 * k + one
+                rows = slice(h * head_dim, (h + 1) * head_dim)
+                met = dyt_ref[part, rows, :].astype(F32) * carried[one * head_dim : (one + 1) * head_dim, :]
+                brought_s[h : h + 1, :] = jnp.sum(met, axis=0, keepdims=True)
+        brought = brought_s[...] * rows_ref[part, 0]
+        later = later_s[:, 0:1]
+        dlog = running_sum(brought, reverse=True) + later
+        later_s[...] = later_s[...] + jnp.sum(brought, axis=1, keepdims=True)
+        dlogits = rows_ref[part, 1] * dlog
+        dlogits_ref[:, here] = dlogits_in[part] - dlogits
+        totals_s[0] -= rows_ref[part, 2] * dlog
+        totals_s[1] -= dlogits
 
     @pl.when(step_id == pl.num_programs(0) - 1)
     def _():
-        sums_ref[...] = jnp.sum(totals_s[...], axis=2)
-
-
-def third_pass(base, dyt, maps, dlogits, sums, rows, own, other, received, sent):
+        sums_ref[...] = jnp.zeros_like(sums_ref)
+        sums = jnp.sum(totals_s[...], axis=2)
+        for which in range(3):
+            row = jnp.broadcast_to(sums[which : which + 1, :], (sums_ref.shape[0], heads))
+            sums_ref[:, which * 32 : which * 32 + heads] = row
+
+
+def third_pass(base, dyt, maps, dlogits, sums, rows, own, other, received, sent, devices):
     groups, width, _ = dyt.shape
     heads = rows.shape[2]
     length = groups * GROUP
     state_n = maps.shape[1] // 2
-    back = lambda i: groups - 1 - i
+    steps = groups // THIRD_BLOCKS
+    back = lambda i: steps - 1 - i
     smem = pl.BlockSpec(memory_space=pltpu.SMEM)
-    per_block = lambda rows, cols: pl.BlockSpec((None, rows, cols), lambda i: (back(i), 0, 0))
+    per_block = lambda rows, cols: pl.BlockSpec(
+        (THIRD_BLOCKS, rows, cols), lambda i: (back(i), 0, 0)
+    )
     whole = lambda rows, cols: pl.BlockSpec((rows, cols), lambda i: (0, 0))
     return pl.pallas_call(
         functools.partial(third_kernel, heads, width // heads),
-        grid=(groups,),
+        grid=(steps,),
         in_specs=[
             smem,
             per_block(width, GROUP),
-            pl.BlockSpec((GROUP, 2 * state_n), lambda i: (back(i), 0)),
+            pl.BlockSpec((THIRD_BLOCKS * GROUP, 2 * state_n), lambda i: (back(i), 0)),
             per_block(heads, GROUP),
             pl.BlockSpec((3, heads, GROUP), lambda i: (0, 0, 0)),
-            pl.BlockSpec((None, 3, heads, GROUP), lambda i: (back(i), 0, 0, 0)),
+            pl.BlockSpec((THIRD_BLOCKS, 3, heads, GROUP), lambda i: (back(i), 0, 0, 0)),
             whole(width // 2, state_n),
             whole(width // 2, state_n),
             whole(width + heads, state_n),
             pl.BlockSpec((heads, state_n), lambda i: (width // heads, 0)),
         ],
         out_specs=[
-            pl.BlockSpec((heads, GROUP), lambda i: (0, back(i))),
-            whole(3, heads),
+            pl.BlockSpec((heads, THIRD_BLOCKS * GROUP), lambda i: (0, back(i))),
+            whole(devices, 128),
             whole(width, state_n),
         ],
         out_shape=[
             jax.ShapeDtypeStruct((heads, length), F32),
-            jax.ShapeDtypeStruct((3, heads), F32),
+            jax.ShapeDtypeStruct((devices, 128), F32),
             jax.ShapeDtypeStruct((width, state_n), BF16),
         ],
         scratch_shapes=[
@@ -583,22 +597,24 @@
         for at in range(0, width, state_n):
             entry_t[:, at : at + state_n] = entry_ref[at : at + state_n, :].T
 
-    c_t = maps_ref[:, state_n:].T
-    for k in range(heads // 2):
-        lo = k * 2 * head_dim
-        carried = dot(entry_ref[lo : lo + 2 * head_dim, :], c_t)
-        ys = []
-        for one in range(2):
-            h = 2 * k + one
-            rows = slice(h * head_dim, (h + 1) * head_dim)
-            reach = rows_ref[0, h : h + 1, :]
-            dyi_s[rows, :] = (dyt_ref[rows, :].astype(F32) * reach).astype(BF16)
-            brought = carried[one * head_dim : (one + 1) * head_dim, :] * reach
-            ys.append((yt_ref[rows, :].astype(F32) + brought).astype(BF16))
-        y_ref[:, lo : lo + 2 * head_dim] = jnp.concatenate(ys, axis=0).T
-    dc_t = dmaps_in[state_n:, :] + dot(entry_t[...], dyi_s[...])
-    dmaps_ref[:, :state_n] = dmaps_in[:state_n, :].T.astype(BF16)
-    dmaps_ref[:, state_n:] = dc_t.T.astype(BF16)
+    for part in range(yt_ref.shape[0]):
+        here = slice(part * GROUP, (part + 1) * GROUP)
+        c_t = maps_ref[here, state_n:].T
+        for k in range(heads // 2):
+            lo = k * 2 * head_dim
+            carried = dot(entry_ref[lo : lo + 2 * head_dim, :], c_t)
+            ys = []
+            for one in range(2):
+                h = 2 * k + one
+                rows = slice(h * head_dim, (h + 1) * head_dim)
+                reach = rows_ref[part, 0, h : h + 1, :]
+                dyi_s[part, rows, :] = (dyt_ref[part, rows, :].astype(F32) * reach).astype(BF16)
+                brought = carried[one * head_dim : (one + 1) * head_dim, :] * reach
+                ys.append((yt_ref[part, rows, :].astype(F32) + brought).astype(BF16))
+            y_ref[here, lo : lo + 2 * head_dim] = jnp.concatenate(ys, axis=0).T
+        dc_t = dmaps_in[part, state_n:, :] + dot(entry_t[...], dyi_s[part])
+        dmaps_ref[here, :state_n] = dmaps_in[part, :state_n, :].T.astype(BF16)
+        dmaps_ref[here, state_n:] = dc_t.T.astype(BF16)
 
 
 def fourth_pass(yt, dyt, maps, dmaps, rows, entry):
@@ -606,21 +622,21 @@
     heads = rows.shape[2]
     length = groups * GROUP
     state_n = maps.shape[1] // 2
-    per_block = lambda rows, cols: pl.BlockSpec((None, rows, cols), lambda i: (i, 0, 0))
+    per_block = lambda rows, cols: pl.BlockSpec((FOURTH_BLOCKS, rows, cols), lambda i: (i, 0, 0))
     return pl.pallas_call(
         functools.partial(fourth_kernel, heads, width // heads),
-        grid=(groups,),
+        grid=(groups // FOURTH_BLOCKS,),
         in_specs=[
             per_block(width, GROUP),
             per_block(width, GROUP),
-            pl.BlockSpec((GROUP, 2 * state_n), lambda i: (i, 0)),
+            pl.BlockSpec((FOURTH_BLOCKS * GROUP, 2 * state_n), lambda i: (i, 0)),
             per_block(2 * state_n, GROUP),
-            pl.BlockSpec((None, 1, heads, GROUP), lambda i: (i, 0, 0, 0)),
+            pl.BlockSpec((FOURTH_BLOCKS, 1, heads, GROUP), lambda i: (i, 0, 0, 0)),
             pl.BlockSpec((width, state_n), lambda i: (0, 0)),
         ],
         out_specs=[
-            pl.BlockSpec((GROUP, width), lambda i: (i, 0)),
-            pl.BlockSpec((GROUP, 2 * state_n), lambda i: (i, 0)),
+            pl.BlockSpec((FOURTH_BLOCKS * GROUP, width), lambda i: (i, 0)),
+            pl.BlockSpec((FOURTH_BLOCKS * GROUP, 2 * state_n), lambda i: (i, 0)),
         ],
         out_shape=[
             jax.ShapeDtypeStruct((length, width), BF16),
@@ -628,7 +644,7 @@
         ],
         scratch_shapes=[
             pltpu.VMEM((state_n, width), BF16),
-            pltpu.VMEM((width, GROUP), BF16),
+            pltpu.VMEM((FOURTH_BLOCKS, width, GROUP), BF16),
         ],
         compiler_params=pltpu.CompilerParams(
             dimension_semantics=("arbitrary",), vmem_limit_bytes=63 << 20
@@ -663,7 +679,7 @@
     x, dy, maps, logits = head_inputs[0], grad_output[0], state_maps[0], step_logits[0]
 
     dealt = lax.all_to_all(old_states[0].reshape(streams, -1), "stream", 0, 0, tiled=True)
-    xt, dyt, states, after, suffix, sent = first_pass(
+    states, after, suffix, sent = first_pass(
         doc_starts, base, x, dy, maps, logits, head_params
     )
     dealt, sent = lax.optimization_barrier((dealt, sent))
@@ -671,21 +687,21 @@
     dealt, received = lax.optimization_barrier((dealt, received))
     own = lax.all_to_all(
         dealt.at[old_owner].get(mode="promise_in_bounds"), "stream", 0, 0, tiled=True)
-    yt, dx, dmaps, dlogits, sums, rows = second_pass(
-        doc_starts, base, skip_gain, x, xt, dyt, maps, logits, head_params,
+    yt, dx, dmaps, dlogits, sums, rows, dyt = second_pass(
+        doc_starts, base, skip_gain, x, dy, maps, logits, head_params,
         states, after, suffix, received,
     )
     own, sums = lax.optimization_barrier((own, sums))
     own = own.reshape(width // 2, state_n)
     other = lax.ppermute(own, "seq", swap)
-    dlogits, sums, entry = third_pass(
-        base, dyt, maps, dlogits, sums, rows, own, other, received, sent
+    devices = streams * lax.axis_size("seq")
+    dlogits, everyone, entry = third_pass(
+        base, dyt, maps, dlogits, sums, rows, own, other, received, sent, devices
     )
-    devices = streams * lax.axis_size("seq")
-    everyone = jnp.broadcast_to(sums.reshape(1, -1), (devices, sums.size))
     gathered = lax.all_to_all(everyone, ("stream", "seq"), 0, 0, tiled=True)
     y, dmaps = fourth_pass(yt, dyt, maps, dmaps, rows, entry)
-    totals = jnp.sum(gathered, axis=0).reshape(sums.shape)
+    totals = jnp.sum(gathered, axis=0)
+    totals = [totals[32 * k : 32 * k + heads] for k in range(3)]
     return (y[None], dx[None], dmaps[None], dlogits[None], totals[0], totals[1], totals[2])
 
 

time: 112 us -> 106 us (0.946)
  Pallas kernels: 67.5 us -> 60.9 us
  waiting for transfers between devices: 4.31 us -> 6.19 us
  local copies, waits for them, and re-layouts: 5.37 us -> 3.97 us
    pallas_call x1, Pallas kernels: 9.21 us -> 6.13 us  [third_pass(): pl.pallas_call(functools.partial(third_kernel, heads, width // heads), gr...]
    pallas_call x1, Pallas kernels: 15.3 us -> 12.8 us  [first_pass(): pl.pallas_call(functools.partial(first_kernel, heads, width // heads), gr...]
    pallas_call x1, Pallas kernels: 9.76 us -> 7.42 us  [fourth_pass(): pl.pallas_call(functools.partial(fourth_kernel, heads, width // heads), g...]
    all_to_all x1, waiting for transfers between devices: 0.01 us -> 1.88 us  [shards(): gathered = lax.all_to_all(everyone, ('stream', 'seq'), 0, 0, tiled=True)]
    broadcast_in_dim x2 -> x0, local copies, waits for them, and re-layouts: 1.4 us -> none  [shards(): everyone = jnp.broadcast_to(sums.reshape(1, -1), (devices, sums.size))]
    pallas_call x1, Pallas kernels: 33.2 us -> 34.6 us  [second_pass(): pl.pallas_call(functools.partial(second_kernel, heads, width // heads), g...]
  transfers between devices with their start and end apart: 5 -> 5, of which waited for: 2 -> 3; matrix products, arithmetic and copies ran while one was open for 2% -> 2% of each run, Pallas kernels for 52% -> 52%
where the time goes in v3:
time: 106 us; the launch traced here: 105 us
  Pallas kernels  60.9 us (57%)
  starting transfers between devices  32.1 us (30%)
  waiting for transfers between devices  6.19 us (6%)
  local copies, waits for them, and re-layouts  3.97 us (4%)
  other arithmetic  1.43 us (1%)
    pallas_call x1, Pallas kernels, second_pass(): pl.pallas_call(functools.partial(second_kernel, heads, width // heads), g...  34.6 us
    pallas_call x1, Pallas kernels, first_pass(): pl.pallas_call(functools.partial(first_kernel, heads, width // heads), gr...  12.8 us
    all_to_all x1, starting transfers between devices, shards(): lax.all_to_all(old_states[0].reshape(streams, -1), 'stream', 0, 0, tiled=...  11.5 us
    all_to_all x1, starting transfers between devices, shards(): lax.all_to_all(dealt.at[old_owner].get(mode='promise_in_bounds'), 'stream...  10.4 us
    all_to_all x1, starting transfers between devices, shards(): gathered = lax.all_to_all(everyone, ('stream', 'seq'), 0, 0, tiled=True)  9.98 us
    pallas_call x1, Pallas kernels, fourth_pass(): pl.pallas_call(functools.partial(fourth_kernel, heads, width // heads), g...  7.42 us
    pallas_call x1, Pallas kernels, third_pass(): pl.pallas_call(functools.partial(third_kernel, heads, width // heads), gr...  6.13 us
    ppermute x1, waiting for transfers between devices, shards(): received = lax.ppermute(sent, 'seq', swap)  2.6 us
  transfers between devices with their start and end apart: 5, of which 3 were waited for; matrix products, arithmetic and copies ran while one was open for 2% of the time, Pallas kernels for 52%

profile of v3, /device:TPU:0, one launch (start us, length us, event | category | flops | bytes accessed | tf_op | source)
XLA Modules:
  0.0 105.3 jit_solution(11824994940607298749)
XLA Ops:
  0.6 11.5 %all-to-all-start = ((f32[64,1,1536]{2,1,0:T(1,128)}), f32[64,1,1536]{2,1,0:T(1,128)S(1)}, u32[]{:S(2)}, u32[]{:S(2)}) async-start(f32[64,1,1536]{2,1,0:T(1,128)} %bitcast.36), calls=%async_computation | async-start | bytes 786432 | tf_op jit(solution)/shard_map/all_to_all | solution.py:681
  12.2 0.7 pad_maximum_fusion
  12.8 0.7 copy.20.heads_ref
  13.5 0.6 add_bitcast_fusion.base_ref
  14.1 0.0 copy-start.2
  14.1 12.8 %first_pass.1 = (bf16[6,1536,128]{2,1,0:T(8,128)(2,1)}, bf16[6,1536,128]{2,1,0:T(8,128)(2,1)}, f32[6,24,128]{2,1,0:T(8,128)}, f32[1560,128]{1,0:T(8,128)}) custom-call(s32[1,2]{1,0:T(1,128)} %doc_ref.3, s32[1,2]{1,0:T(1,128)} %add_bitcast_fusion.base_ref, bf16[1536,1536]{1,0:T(8,128)(2,1)} %bitcast.30, bf16[1536,1536]{1,0:T(8,128)(2,1)} %bitcast.32, ...), custom_call_target="tpu_custom_call" | custom-call | flops 1207959552 | bytes 28311552 | tf_op jit(solution)/shard_map/first_pass/pallas_call | solution.py:152
  26.9 0.0 all-to-all-done
  27.0 0.1 collective-permute-start
  27.1 0.0 copy-done.2
  27.1 2.6 %collective-permute-done.exit_ref.received_ref = f32[1560,128]{1,0:T(8,128)} collective-permute-done((f32[1560,128]{1,0:T(8,128)}, f32[1560,128]{1,0:T(8,128)}, u32[]{:S(2)}, u32[]{:S(2)}) %collective-permute-start) | collective-permute-done | bytes 798752 | tf_op jit(solution)/shard_map/ppermute | solution.py:686
  29.7 0.7 gather_fusion
  30.4 1.2 %copy.21 = f32[64,1,1536]{2,1,0:T(1,128)} copy(f32[64,1,1536]{2,0,1:T(8,128)S(1)} %bitcast.35) | data formatting | bytes 786432 | tf_op jit(solution)/shard_map/all_to_all | solution.py:688
  31.6 10.4 %all-to-all-start.1 = ((f32[64,1,1536]{2,1,0:T(1,128)}), f32[64,1,1536]{2,1,0:T(1,128)S(1)}, u32[]{:S(2)}, u32[]{:S(2)}) async-start(f32[64,1,1536]{2,1,0:T(1,128)} %copy.21), calls=%async_computation.1 | async-start | bytes 786432 | tf_op jit(solution)/shard_map/all_to_all | solution.py:688
  42.0 34.6 %second_pass.1 = (bf16[6,1536,256]{2,1,0:T(8,128)(2,1)}, bf16[1536,1536]{1,0:T(8,128)(2,1)}, f32[6,256,256]{2,1,0:T(8,128)}, f32[6,24,256]{2,1,0:T(8,128)}, f32[...) custom-call(s32[1,2]{1,0:T(1,128)} %doc_ref.3, s32[1,2]{1,0:T(1,128)} %add_bitcast_fusion.base_ref, ...), custom_call_target="tpu_custom_call" | custom-call | flops 6039797760 | bytes 33030144 | tf_op jit(solution)/shard_map/second_pass/pallas_call | solution.py:397
  76.5 0.0 all-to-all-done.1
  76.6 0.0 copy-start
  76.6 0.1 collective-permute-start.1
  76.7 1.7 %collective-permute-done.1.other_ref = f32[768,128]{1,0:T(8,128)S(1)} collective-permute-done((f32[768,128]{1,0:T(8,128)S(1)}, f32[768,128]{1,0:T(8,128)S(1)}, u32[]{:S(2)}, u32[]{:S(2)}) %collective-permute-start.1) | collective-permute-done | bytes 393248 | tf_op jit(solution)/shard_map/ppermute | solution.py:696
  78.4 0.0 copy-start.1
  78.4 0.0 copy-done
  78.4 0.7 copy-done.1
  79.2 6.1 %third_pass.1 = (f32[24,1536]{1,0:T(8,128)}, f32[128,128]{1,0:T(8,128)}, bf16[1536,128]{1,0:T(8,128)(2,1)}) custom-call(s32[1,2]{1,0:T(1,128)} %add_bitcast_fusion.base_ref, bf16[6,1536,256]{2,1,0:T(8,128)(2,1)} %get-tuple-element.37.dyt_ref, bf16[1536,256]{1,0:T(8,128)(2,1)} %bitcast.28, f32[6,24,256]{2,1,0:T(8,128)} %get-tuple-element.40.dlogits_in, ...), custom_call_target="tpu_custom_call" | custom-call | flops 603979776 | bytes 4718592 | tf_op jit(solution)/shard_map/third_pass/pallas_call | solution.py:549
  85.3 10.0 %all-to-all-start.2 = ((f32[128,1,128]{2,1,0:T(1,128)}), f32[128,1,128]{2,1,0:T(1,128)S(1)}, u32[]{:S(2)}, u32[]{:S(2)}) async-start(f32[128,1,128]{2,1,0:T(1,128)} %bitcast.39), calls=%async_computation.2 | async-start | bytes 131072 | tf_op jit(solution)/shard_map/all_to_all | solution.py:701
  95.3 7.4 %fourth_pass.1 = (bf16[1536,1536]{1,0:T(8,128)(2,1)}, bf16[1536,256]{1,0:T(8,128)(2,1)}) custom-call(bf16[6,1536,256]{2,1,0:T(8,128)(2,1)} %get-tuple-element.36.yt_ref, bf16[6,1536,256]{2,1,0:T(8,128)(2,1)} %get-tuple-element.37.dyt_ref, bf16[1536,256]{1,0:T(8,128)(2,1)} %bitcast.29, f32[6,256,256]{2,1,0:T(8,128)} %get-tuple-element.38.dmaps_in, ...), custom_call_target="tpu_custom_call" | custom-call | flops 1207959552 | bytes 14155776 | tf_op jit(solution)/shard_map/fourth_pass/pallas_call | solution.py:626
  102.7 1.9 %all-to-all-done.2 = f32[128,1,128]{2,1,0:T(1,128)S(1)} async-done(((f32[128,1,128]{2,1,0:T(1,128)}), f32[128,1,128]{2,1,0:T(1,128)S(1)}, u32[]{:S(2)}, u32[]{:S(2)}) %all-to-all-start.2) | async-done | bytes 65568 | tf_op jit(solution)/shard_map/all_to_all | solution.py:701
  104.6 0.2 reduce_sum.9
  104.8 0.6 fusion
  (5 shorter events, 0.1 us)
Async XLA Ops:
  0.6 26.3 %all-to-all-start = ((f32[64,1,1536]{2,1,0:T(1,128)}), f32[64,1,1536]{2,1,0:T(1,128)S(1)}, u32[]{:S(2)}, u32[]{:S(2)}) async-start(f32[64,1,1536]{2,1,0:T(1,128)} %bitcast.36), calls=%async_computation | async-start | bytes 786432 | tf_op jit(solution)/shard_map/all_to_all | solution.py:681
  14.1 13.0 %copy-start.2 = (s32[64]{0:T(128)S(1)}, s32[64]{0:T(128)}, u32[]{:S(2)}) copy-start(s32[64]{0:T(128)} %param.17) | copy-start | bytes 772
  27.0 2.7 %collective-permute-start = (f32[1560,128]{1,0:T(8,128)}, f32[1560,128]{1,0:T(8,128)}, u32[]{:S(2)}, u32[]{:S(2)}) collective-permute-start(f32[1560,128]{1,0:T(8,128)} %get-tuple-element.34.total_ref), channel_id=1, source_target_pairs={{0,1},{1,0},{2,3},{3,2},{4,5},{5,4},{6,7},{7,6},{8,9},{9,8},{10,11... | collective-permute-start | bytes 2396168 | tf_op jit(solution)/shard_map/ppermute | solution.py:686
  31.6 45.0 %all-to-all-start.1 = ((f32[64,1,1536]{2,1,0:T(1,128)}), f32[64,1,1536]{2,1,0:T(1,128)S(1)}, u32[]{:S(2)}, u32[]{:S(2)}) async-start(f32[64,1,1536]{2,1,0:T(1,128)} %copy.21), calls=%async_computation.1 | async-start | bytes 786432 | tf_op jit(solution)/shard_map/all_to_all | solution.py:688
  76.6 1.8 %copy-start = (f32[768,128]{1,0:T(8,128)}, f32[768,128]{1,0:T(8,128)S(1)}, u32[]{:S(2)}) copy-start(f32[768,128]{1,0:T(8,128)S(1)} %reshape.28.own_ref) | copy-start | bytes 1179652
  76.6 1.8 %collective-permute-start.1 = (f32[768,128]{1,0:T(8,128)S(1)}, f32[768,128]{1,0:T(8,128)S(1)}, u32[]{:S(2)}, u32[]{:S(2)}) collective-permute-start(f32[768,128]{1,0:T(8,128)S(1)} %reshape.28.own_ref), channel_id=1, source_target_pairs={{0,1},{1,0},{2,3},{3,2},{4,5},{5,4},{6,7},{7,6},{8,9},{9,8},{10,11... | collective-permute-start | bytes 1179656 | tf_op jit(solution)/shard_map/ppermute | solution.py:696
  78.4 0.7 copy-start.1
  85.3 19.3 %all-to-all-start.2 = ((f32[128,1,128]{2,1,0:T(1,128)}), f32[128,1,128]{2,1,0:T(1,128)S(1)}, u32[]{:S(2)}, u32[]{:S(2)}) async-start(f32[128,1,128]{2,1,0:T(1,128)} %bitcast.39), calls=%async_computation.2 | async-start | bytes 131072 | tf_op jit(solution)/shard_map/all_to_all | solution.py:701

commit v4 on v3

--- a/solution.py
+++ b/solution.py
@@ -8,6 +8,7 @@
 from jax.sharding import PartitionSpec as P
 
 GROUP = 256
+TERMS = 7
 THIRD_BLOCKS = 6
 FOURTH_BLOCKS = 3
 LOG2E = 1.4426950408889634
@@ -24,11 +25,11 @@
 
 def running_sum(v, reverse=False):
     size = v.shape[1]
-    lane = lax.broadcasted_iota(jnp.int32, v.shape, 1)
+    lane = lax.broadcasted_iota(jnp.int32, v.shape, 1) % GROUP
     by = 1
-    while by < size:
+    while by < GROUP:
         if reverse:
-            v = v + jnp.where(lane < size - by, pltpu.roll(v, size - by, 1), 0.0)
+            v = v + jnp.where(lane < GROUP - by, pltpu.roll(v, size - by, 1), 0.0)
         else:
             v = v + jnp.where(lane >= by, pltpu.roll(v, by, 1), 0.0)
         by *= 2
@@ -53,19 +54,38 @@
     return total
 
 
-def block_terms(logits, heads_ref, found, first):
-    shifted = logits + heads_ref[:, 1:2]
+def column(ref, heads):
+    row = lax.broadcasted_iota(jnp.int32, (heads, 1), 0)
+    values = jnp.zeros((heads, 1), F32)
+    for h in range(heads):
+        values = jnp.where(row == h, ref[h], values)
+    return values
+
+
+def write_terms(doc_ref, base, logits, log_rates, bias, terms_ref, decays_ref):
+    shifted = logits + bias
     step = jnp.maximum(shifted, 0.0) + jnp.log1p(jnp.exp(-jnp.abs(shifted)))
-    rate = jnp.exp(heads_ref[:, 0:1])
+    rate = jnp.exp(log_rates)
+    slope = jax.nn.sigmoid(shifted)
     cum = running_sum(-step * rate)
-    end = cum[:, GROUP - 1 : GROUP]
-    position = first + lax.broadcasted_iota(jnp.int32, (1, GROUP), 1)
-    doc = doc_count(found, position)
-    docs = sum(inside for inside, _ in found)
-    inflow = jnp.where(doc == 0, jnp.exp(cum), 0.0)
-    weight = jnp.where(doc == docs, jnp.exp(end - cum), 0.0) * step
-    decay = jnp.where(docs == 0, jnp.exp(end), 0.0)
-    return shifted, step, rate, cum, doc, inflow, weight, decay
+    over = cum * LOG2E
+    terms_ref[0] = over
+    terms_ref[1] = over - jnp.log2(step)
+    terms_ref[4] = slope / step
+    terms_ref[5] = rate * slope
+    terms_ref[6] = step * rate
+    for block in range(logits.shape[1] // GROUP):
+        here = slice(block * GROUP, (block + 1) * GROUP)
+        first = base + block * GROUP
+        found = starts_in(doc_ref, first)
+        doc = doc_count(found, first + lax.broadcasted_iota(jnp.int32, (1, GROUP), 1))
+        docs = sum(inside for inside, _ in found)
+        inner = cum[:, here]
+        end = inner[:, GROUP - 1 : GROUP]
+        terms_ref[2, :, here] = jnp.where(doc == 0, jnp.exp(inner), 0.0)
+        terms_ref[3, :, here] = jnp.where(doc == docs, jnp.exp(end - inner), 0.0) * step[:, here]
+        decay = jnp.where(docs == 0, jnp.exp(end), 0.0)
+        decays_ref[block] = jnp.broadcast_to(decay, decays_ref.shape[1:])
 
 
 def first_kernel(
@@ -77,11 +97,14 @@
     dy_ref,
     maps_ref,
     logits_ref,
-    heads_ref,
+    rates_ref,
+    bias_ref,
     states_ref,
     after_ref,
     suffix_ref,
     sent_ref,
+    terms_ref,
+    decays_ref,
     xt_ref,
     dyt_ref,
     local_ref,
@@ -93,20 +116,22 @@
 ):
     step_id = pl.program_id(0)
     block = pl.num_programs(0) - 1 - step_id
-    first = base_ref[0, 0] + block * GROUP
     state_n = maps_ref.shape[1] // 2
 
     @pl.when(step_id == 0)
     def _():
+        log_rates, bias = column(rates_ref, heads), column(bias_ref, heads)
+        write_terms(
+            doc_ref, base_ref[0, 0], logits_ref[...], log_rates, bias, terms_ref, decays_ref
+        )
         local_ref[...] = jnp.zeros_like(local_ref)
         grad_ref[...] = jnp.zeros_like(grad_ref)
         total_ref[...] = jnp.ones_like(total_ref)
 
-    found = starts_in(doc_ref, first)
-    _, _, _, _, _, inflow, weight, decay = block_terms(logits_ref[...], heads_ref, found, first)
-    weight_s[...] = weight
-    inflow_s[...] = inflow
-    decay_s[...] = jnp.broadcast_to(decay, decay_s.shape)
+    here = pl.ds(pl.multiple_of(block * GROUP, GROUP), GROUP)
+    weight_s[...] = terms_ref[3, :, here]
+    inflow_s[...] = terms_ref[2, :, here]
+    decay_s[...] = decays_ref[block]
     suffix_ref[...] = total_ref[...]
     b_part = maps_ref[:, :state_n]
     c_part = maps_ref[:, state_n:]
@@ -140,7 +165,7 @@
         sent_ref[width:, :] = total_ref[...]
 
 
-def first_pass(doc, base, x, dy, maps, logits, head_params):
+def first_pass(doc, base, x, dy, maps, logits, log_rates, step_bias):
     length, width = x.shape
     heads = logits.shape[0]
     state_n = maps.shape[1] // 2
@@ -158,20 +183,25 @@
             pl.BlockSpec((GROUP, width), lambda i: (back(i), 0)),
             pl.BlockSpec((GROUP, width), lambda i: (back(i), 0)),
             pl.BlockSpec((GROUP, 2 * state_n), lambda i: (back(i), 0)),
-            pl.BlockSpec((heads, GROUP), lambda i: (0, back(i))),
-            whole(heads, head_params.shape[1]),
+            whole(heads, length),
+            smem,
+            smem,
         ],
         out_specs=[
             per_block(width, state_n),
             per_block(width, state_n),
             per_block(heads, state_n),
             whole(width + heads, state_n),
+            pl.BlockSpec((TERMS, heads, length), lambda i: (0, 0, 0)),
+            pl.BlockSpec((groups, heads, state_n), lambda i: (0, 0, 0)),
         ],
         out_shape=[
             jax.ShapeDtypeStruct((groups, width, state_n), BF16),
             jax.ShapeDtypeStruct((groups, width, state_n), BF16),
             jax.ShapeDtypeStruct((groups, heads, state_n), F32),
             jax.ShapeDtypeStruct((width + heads, state_n), F32),
+            jax.ShapeDtypeStruct((TERMS, heads, length), F32),
+            jax.ShapeDtypeStruct((groups, heads, state_n), F32),
         ],
         scratch_shapes=[
             pltpu.VMEM((width, GROUP), BF16),
@@ -192,7 +222,7 @@
             transcendentals=4 * heads * length,
         ),
         name="first_pass",
-    )(doc, base, x, dy, maps, logits, head_params)
+    )(doc, base, x, dy, maps, logits, log_rates, step_bias)
 
 
 def second_kernel(
@@ -204,8 +234,8 @@
     x_ref,
     dy_ref,
     maps_ref,
-    logits_ref,
-    heads_ref,
+    terms_ref,
+    decays_ref,
     states_ref,
     after_ref,
     suffix_ref,
@@ -251,18 +281,17 @@
         mix_s[...] = jnp.zeros_like(mix_s)
 
     found = starts_in(doc_ref, first)
-    shifted, step, rate, cum, doc, inflow, weight, decay = block_terms(
-        logits_ref[...], heads_ref, found, first
-    )
-    weight_s[...] = weight
+    doc = doc_count(found, first + lax.broadcasted_iota(jnp.int32, (1, GROUP), 1))
+    inflow = terms_ref[2]
+    weight_s[...] = terms_ref[3]
     inflow_s[...] = inflow
-    decay_s[...] = jnp.broadcast_to(decay, decay_s.shape)
+    decay_s[...] = decays_ref[...]
+    decay = decays_ref[:, 0:1]
     rows_ref[0] = inflow * prefix_s[:, 0:1]
     prefix_s[...] = prefix_s[...] * decay
     last = base_ref[0, 1].astype(F32)
-    over = cum * LOG2E
-    over_s[...] = over
-    under = over - jnp.log2(step)
+    over_s[...] = terms_ref[0]
+    under = terms_ref[1]
     pad = jnp.zeros((half - heads, GROUP), F32)
     under_t = jnp.concatenate([under, pad], axis=0).T
     for h in range(heads):
@@ -372,22 +401,20 @@
     given_sum = given_s[...]
     before = jnp.where(lane > 0, pltpu.roll(running_sum(given_sum), 1, 1), 0.0)
     dlog = running_sum(out_s[...] - inner, reverse=True) + before + ends
-    dstep = (inner + given_sum) / step - rate * dlog
-    slope = jax.nn.sigmoid(shifted)
-    dlogits = dstep * slope
+    dlogits = (inner + given_sum) * terms_ref[4] - terms_ref[5] * dlog
     dlogits_ref[...] = dlogits
-    rows_ref[1] = rate * slope
-    rows_ref[2] = step * rate
-    sums_ref[0] += -step * rate * dlog
+    rows_ref[1] = terms_ref[5]
+    rows_ref[2] = terms_ref[6]
+    sums_ref[0] -= terms_ref[6] * dlog
     sums_ref[1] += dlogits
     sums_ref[2] += skip_s[...]
 
 
 def second_pass(
-    doc, base, skip_gain, x, dy, maps, logits, head_params, states, after, suffix, received
+    doc, base, skip_gain, x, dy, maps, terms, decays, states, after, suffix, received
 ):
     length, width = x.shape
-    heads = logits.shape[0]
+    heads = terms.shape[1]
     state_n = maps.shape[1] // 2
     groups = length // GROUP
     half = GROUP // 2
@@ -404,8 +431,8 @@
             pl.BlockSpec((GROUP, width), lambda i: (i, 0)),
             pl.BlockSpec((GROUP, width), lambda i: (i, 0)),
             pl.BlockSpec((GROUP, 2 * state_n), lambda i: (i, 0)),
-            pl.BlockSpec((heads, GROUP), lambda i: (0, i)),
-            whole(heads, head_params.shape[1]),
+            pl.BlockSpec((TERMS, heads, GROUP), lambda i: (0, 0, i)),
+            per_block(heads, state_n),
             per_block(width, state_n),
             per_block(width, state_n),
             per_block(heads, state_n),
@@ -460,7 +487,7 @@
             transcendentals=heads * length * GROUP,
         ),
         name="second_pass",
-    )(doc, base, skip_gain, x, dy, maps, logits, head_params, states, after, suffix, received)
+    )(doc, base, skip_gain, x, dy, maps, terms, decays, states, after, suffix, received)
 
 
 def third_kernel(
@@ -675,12 +702,11 @@
     streams = lax.axis_size("stream")
     swap = [(0, 1), (1, 0)]
     base = jnp.stack([seq_index * length, 1 - seq_index]).astype(jnp.int32).reshape(1, 2)
-    head_params = jnp.stack([log_rates, step_bias], axis=1)
     x, dy, maps, logits = head_inputs[0], grad_output[0], state_maps[0], step_logits[0]
 
     dealt = lax.all_to_all(old_states[0].reshape(streams, -1), "stream", 0, 0, tiled=True)
-    states, after, suffix, sent = first_pass(
-        doc_starts, base, x, dy, maps, logits, head_params
+    states, after, suffix, sent, terms, decays = first_pass(
+        doc_starts, base, x, dy, maps, logits, log_rates, step_bias
     )
     dealt, sent = lax.optimization_barrier((dealt, sent))
     received = lax.ppermute(sent, "seq", swap)
@@ -688,7 +714,7 @@
     own = lax.all_to_all(
         dealt.at[old_owner].get(mode="promise_in_bounds"), "stream", 0, 0, tiled=True)
     yt, dx, dmaps, dlogits, sums, rows, dyt = second_pass(
-        doc_starts, base, skip_gain, x, dy, maps, logits, head_params,
+        doc_starts, base, skip_gain, x, dy, maps, terms, decays,
         states, after, suffix, received,
     )
     own, sums = lax.optimization_barrier((own, sums))

time: 106 us -> 99.2 us (0.936)
  Pallas kernels: 60.9 us -> 55.1 us
    pallas_call x1, Pallas kernels: 34.6 us -> 30 us  [second_pass(): pl.pallas_call(functools.partial(second_kernel, heads, width // heads), g...]
    pallas_call x1, Pallas kernels: 12.8 us -> 11.6 us  [first_pass(): pl.pallas_call(functools.partial(first_kernel, heads, width // heads), gr...]
  transfers between devices with their start and end apart: 5 -> 5, of which waited for: 3 -> 3; matrix products, arithmetic and copies ran while one was open for 2% -> 1% of each run, Pallas kernels for 52% -> 50%
where the time goes in v4:
time: 99.2 us; the launch traced here: 98.1 us
  Pallas kernels  55.1 us (56%)
  starting transfers between devices  32 us (32%)
  waiting for transfers between devices  6.21 us (6%)
  local copies, waits for them, and re-layouts  3.29 us (3%)
    pallas_call x1, Pallas kernels, second_pass(): pl.pallas_call(functools.partial(second_kernel, heads, width // heads), g...  30 us
    pallas_call x1, Pallas kernels, first_pass(): pl.pallas_call(functools.partial(first_kernel, heads, width // heads), gr...  11.6 us
    all_to_all x1, starting transfers between devices, shards(): lax.all_to_all(old_states[0].reshape(streams, -1), 'stream', 0, 0, tiled=...  11.5 us
    all_to_all x1, starting transfers between devices, shards(): lax.all_to_all(dealt.at[old_owner].get(mode='promise_in_bounds'), 'stream...  10.3 us
    all_to_all x1, starting transfers between devices, shards(): gathered = lax.all_to_all(everyone, ('stream', 'seq'), 0, 0, tiled=True)  9.99 us
    pallas_call x1, Pallas kernels, fourth_pass(): pl.pallas_call(functools.partial(fourth_kernel, heads, width // heads), g...  7.39 us
    pallas_call x1, Pallas kernels, third_pass(): pl.pallas_call(functools.partial(third_kernel, heads, width // heads), gr...  6.11 us
    ppermute x1, waiting for transfers between devices, shards(): received = lax.ppermute(sent, 'seq', swap)  2.6 us
  transfers between devices with their start and end apart: 5, of which 3 were waited for; matrix products, arithmetic and copies ran while one was open for 1% of the time, Pallas kernels for 50%

profile of v4, /device:TPU:0, one launch (start us, length us, event | category | flops | bytes accessed | tf_op | source)
XLA Modules:
  0.0 98.1 jit_solution(9169991103095787028)
XLA Ops:
  0.6 11.5 %all-to-all-start = ((f32[64,1,1536]{2,1,0:T(1,128)}), f32[64,1,1536]{2,1,0:T(1,128)S(1)}, u32[]{:S(2)}, u32[]{:S(2)}) async-start(f32[64,1,1536]{2,1,0:T(1,128)} %bitcast.34), calls=%async_computation | async-start | bytes 786432 | tf_op jit(solution)/shard_map/all_to_all | solution.py:707
  12.2 0.6 add_bitcast_fusion.base_ref
  12.7 0.0 copy-start.2
  12.7 11.6 %first_pass.1 = (bf16[6,1536,128]{2,1,0:T(8,128)(2,1)}, bf16[6,1536,128]{2,1,0:T(8,128)(2,1)}, f32[6,24,128]{2,1,0:T(8,128)}, f32[1560,128]{1,0:T(8,128)}, f32[7...) custom-call(s32[1,2]{1,0:T(1,128)} %doc_ref.3, s32[1,2]{1,0:T(1,128)} %add_bitcast_fusion.base_ref, bf16[1536,1536]{1,0:T(8,128)(2,1)} %bitcast.28, ...), custom_call_target="tpu_custom_call" | custom-call | flops 1207959552 | bytes 28311552 | tf_op jit(solution)/shard_map/first_pass/pallas_call | solution.py:177
  24.3 0.0 all-to-all-done
  24.4 0.1 collective-permute-start
  24.5 0.0 copy-done.2
  24.5 2.6 %collective-permute-done.exit_ref.received_ref = f32[1560,128]{1,0:T(8,128)} collective-permute-done((f32[1560,128]{1,0:T(8,128)}, f32[1560,128]{1,0:T(8,128)}, u32[]{:S(2)}, u32[]{:S(2)}) %collective-permute-start) | collective-permute-done | bytes 798752 | tf_op jit(solution)/shard_map/ppermute | solution.py:712
  27.1 0.7 gather_fusion
  27.8 1.2 %copy.17 = f32[64,1,1536]{2,1,0:T(1,128)} copy(f32[64,1,1536]{2,0,1:T(8,128)S(1)} %bitcast.33) | data formatting | bytes 786432 | tf_op jit(solution)/shard_map/all_to_all | solution.py:714
  29.0 10.3 %all-to-all-start.1 = ((f32[64,1,1536]{2,1,0:T(1,128)}), f32[64,1,1536]{2,1,0:T(1,128)S(1)}, u32[]{:S(2)}, u32[]{:S(2)}) async-start(f32[64,1,1536]{2,1,0:T(1,128)} %copy.17), calls=%async_computation.1 | async-start | bytes 786432 | tf_op jit(solution)/shard_map/all_to_all | solution.py:714
  39.3 30.0 %second_pass.1 = (bf16[6,1536,256]{2,1,0:T(8,128)(2,1)}, bf16[1536,1536]{1,0:T(8,128)(2,1)}, f32[6,256,256]{2,1,0:T(8,128)}, f32[6,24,256]{2,1,0:T(8,128)}, f32[...) custom-call(s32[1,2]{1,0:T(1,128)} %doc_ref.3, s32[1,2]{1,0:T(1,128)} %add_bitcast_fusion.base_ref, ...), custom_call_target="tpu_custom_call" | custom-call | flops 6039797760 | bytes 33030144 | tf_op jit(solution)/shard_map/second_pass/pallas_call | solution.py:424
  69.3 0.0 all-to-all-done.1
  69.4 0.0 copy-start
  69.4 0.1 collective-permute-start.1
  69.5 1.7 %collective-permute-done.1.other_ref = f32[768,128]{1,0:T(8,128)S(1)} collective-permute-done((f32[768,128]{1,0:T(8,128)S(1)}, f32[768,128]{1,0:T(8,128)S(1)}, u32[]{:S(2)}, u32[]{:S(2)}) %collective-permute-start.1) | collective-permute-done | bytes 393248 | tf_op jit(solution)/shard_map/ppermute | solution.py:722
  71.2 0.0 copy-start.1
  71.2 0.0 copy-done
  71.2 0.7 copy-done.1
  71.9 6.1 %third_pass.1 = (f32[24,1536]{1,0:T(8,128)}, f32[128,128]{1,0:T(8,128)}, bf16[1536,128]{1,0:T(8,128)(2,1)}) custom-call(s32[1,2]{1,0:T(1,128)} %add_bitcast_fusion.base_ref, bf16[6,1536,256]{2,1,0:T(8,128)(2,1)} %get-tuple-element.41.dyt_ref, bf16[1536,256]{1,0:T(8,128)(2,1)} %bitcast.26, f32[6,24,256]{2,1,0:T(8,128)} %get-tuple-element.44.dlogits_in, ...), custom_call_target="tpu_custom_call" | custom-call | flops 603979776 | bytes 4718592 | tf_op jit(solution)/shard_map/third_pass/pallas_call | solution.py:576
  78.1 10.0 %all-to-all-start.2 = ((f32[128,1,128]{2,1,0:T(1,128)}), f32[128,1,128]{2,1,0:T(1,128)S(1)}, u32[]{:S(2)}, u32[]{:S(2)}) async-start(f32[128,1,128]{2,1,0:T(1,128)} %bitcast.36), calls=%async_computation.2 | async-start | bytes 131072 | tf_op jit(solution)/shard_map/all_to_all | solution.py:727
  88.0 7.4 %fourth_pass.1 = (bf16[1536,1536]{1,0:T(8,128)(2,1)}, bf16[1536,256]{1,0:T(8,128)(2,1)}) custom-call(bf16[6,1536,256]{2,1,0:T(8,128)(2,1)} %get-tuple-element.40.yt_ref, bf16[6,1536,256]{2,1,0:T(8,128)(2,1)} %get-tuple-element.41.dyt_ref, bf16[1536,256]{1,0:T(8,128)(2,1)} %bitcast.27, f32[6,256,256]{2,1,0:T(8,128)} %get-tuple-element.42.dmaps_in, ...), custom_call_target="tpu_custom_call" | custom-call | flops 1207959552 | bytes 14155776 | tf_op jit(solution)/shard_map/fourth_pass/pallas_call | solution.py:653
  95.4 1.9 %all-to-all-done.2 = f32[128,1,128]{2,1,0:T(1,128)S(1)} async-done(((f32[128,1,128]{2,1,0:T(1,128)}), f32[128,1,128]{2,1,0:T(1,128)S(1)}, u32[]{:S(2)}, u32[]{:S(2)}) %all-to-all-start.2) | async-done | bytes 65568 | tf_op jit(solution)/shard_map/all_to_all | solution.py:727
  97.3 0.2 reduce_sum.9
  97.5 0.6 fusion
  (5 shorter events, 0.1 us)
Async XLA Ops:
  0.6 23.7 %all-to-all-start = ((f32[64,1,1536]{2,1,0:T(1,128)}), f32[64,1,1536]{2,1,0:T(1,128)S(1)}, u32[]{:S(2)}, u32[]{:S(2)}) async-start(f32[64,1,1536]{2,1,0:T(1,128)} %bitcast.34), calls=%async_computation | async-start | bytes 786432 | tf_op jit(solution)/shard_map/all_to_all | solution.py:707
  12.7 11.7 %copy-start.2 = (s32[64]{0:T(128)S(1)}, s32[64]{0:T(128)}, u32[]{:S(2)}) copy-start(s32[64]{0:T(128)} %param.17) | copy-start | bytes 772
  24.4 2.7 %collective-permute-start = (f32[1560,128]{1,0:T(8,128)}, f32[1560,128]{1,0:T(8,128)}, u32[]{:S(2)}, u32[]{:S(2)}) collective-permute-start(f32[1560,128]{1,0:T(8,128)} %get-tuple-element.38.total_ref), channel_id=1, source_target_pairs={{0,1},{1,0},{2,3},{3,2},{4,5},{5,4},{6,7},{7,6},{8,9},{9,8},{10,11... | collective-permute-start | bytes 2396168 | tf_op jit(solution)/shard_map/ppermute | solution.py:712
  29.0 40.3 %all-to-all-start.1 = ((f32[64,1,1536]{2,1,0:T(1,128)}), f32[64,1,1536]{2,1,0:T(1,128)S(1)}, u32[]{:S(2)}, u32[]{:S(2)}) async-start(f32[64,1,1536]{2,1,0:T(1,128)} %copy.17), calls=%async_computation.1 | async-start | bytes 786432 | tf_op jit(solution)/shard_map/all_to_all | solution.py:714
  69.4 1.8 %copy-start = (f32[768,128]{1,0:T(8,128)}, f32[768,128]{1,0:T(8,128)S(1)}, u32[]{:S(2)}) copy-start(f32[768,128]{1,0:T(8,128)S(1)} %reshape.28.own_ref) | copy-start | bytes 1179652
  69.4 1.8 %collective-permute-start.1 = (f32[768,128]{1,0:T(8,128)S(1)}, f32[768,128]{1,0:T(8,128)S(1)}, u32[]{:S(2)}, u32[]{:S(2)}) collective-permute-start(f32[768,128]{1,0:T(8,128)S(1)} %reshape.28.own_ref), channel_id=1, source_target_pairs={{0,1},{1,0},{2,3},{3,2},{4,5},{5,4},{6,7},{7,6},{8,9},{9,8},{10,11... | collective-permute-start | bytes 1179656 | tf_op jit(solution)/shard_map/ppermute | solution.py:722
  71.2 0.7 copy-start.1
  78.1 19.3 %all-to-all-start.2 = ((f32[128,1,128]{2,1,0:T(1,128)}), f32[128,1,128]{2,1,0:T(1,128)S(1)}, u32[]{:S(2)}, u32[]{:S(2)}) async-start(f32[128,1,128]{2,1,0:T(1,128)} %bitcast.36), calls=%async_computation.2 | async-start | bytes 131072 | tf_op jit(solution)/shard_map/all_to_all | solution.py:727

commit v5 on v4

--- a/solution.py
+++ b/solution.py
@@ -399,14 +399,11 @@
     ends = decay * jnp.sum(ends_s[...], axis=1, keepdims=True)
     inner = in_s[...]
     given_sum = given_s[...]
-    before = jnp.where(lane > 0, pltpu.roll(running_sum(given_sum), 1, 1), 0.0)
-    dlog = running_sum(out_s[...] - inner, reverse=True) + before + ends
-    dlogits = (inner + given_sum) * terms_ref[4] - terms_ref[5] * dlog
-    dlogits_ref[...] = dlogits
+    rows_ref[3] = out_s[...] - inner
+    rows_ref[4] = jnp.where(lane > 0, pltpu.roll(given_sum, 1, 1), ends)
+    dlogits_ref[...] = (inner + given_sum) * terms_ref[4]
     rows_ref[1] = terms_ref[5]
     rows_ref[2] = terms_ref[6]
-    sums_ref[0] -= terms_ref[6] * dlog
-    sums_ref[1] += dlogits
     sums_ref[2] += skip_s[...]
 
 
@@ -444,7 +441,7 @@
             per_block(2 * state_n, GROUP),
             per_block(heads, GROUP),
             pl.BlockSpec((3, heads, GROUP), lambda i: (0, 0, 0)),
-            pl.BlockSpec((None, 3, heads, GROUP), lambda i: (i, 0, 0, 0)),
+            pl.BlockSpec((None, 5, heads, GROUP), lambda i: (i, 0, 0, 0)),
             per_block(width, GROUP),
         ],
         out_shape=[
@@ -453,7 +450,7 @@
             jax.ShapeDtypeStruct((groups, 2 * state_n, GROUP), F32),
             jax.ShapeDtypeStruct((groups, heads, GROUP), F32),
             jax.ShapeDtypeStruct((3, heads, GROUP), F32),
-            jax.ShapeDtypeStruct((groups, 3, heads, GROUP), F32),
+            jax.ShapeDtypeStruct((groups, 5, heads, GROUP), F32),
             jax.ShapeDtypeStruct((groups, width, GROUP), BF16),
         ],
         scratch_shapes=[
@@ -545,12 +542,13 @@
                 brought_s[h : h + 1, :] = jnp.sum(met, axis=0, keepdims=True)
         brought = brought_s[...] * rows_ref[part, 0]
         later = later_s[:, 0:1]
-        dlog = running_sum(brought, reverse=True) + later
+        dlog = running_sum(brought + rows_ref[part, 3], reverse=True)
+        dlog += running_sum(rows_ref[part, 4]) + later
         later_s[...] = later_s[...] + jnp.sum(brought, axis=1, keepdims=True)
-        dlogits = rows_ref[part, 1] * dlog
-        dlogits_ref[:, here] = dlogits_in[part] - dlogits
+        dlogits = dlogits_in[part] - rows_ref[part, 1] * dlog
+        dlogits_ref[:, here] = dlogits
         totals_s[0] -= rows_ref[part, 2] * dlog
-        totals_s[1] -= dlogits
+        totals_s[1] += dlogits
 
     @pl.when(step_id == pl.num_programs(0) - 1)
     def _():
@@ -582,7 +580,7 @@
             pl.BlockSpec((THIRD_BLOCKS * GROUP, 2 * state_n), lambda i: (back(i), 0)),
             per_block(heads, GROUP),
             pl.BlockSpec((3, heads, GROUP), lambda i: (0, 0, 0)),
-            pl.BlockSpec((THIRD_BLOCKS, 3, heads, GROUP), lambda i: (back(i), 0, 0, 0)),
+            pl.BlockSpec((THIRD_BLOCKS, 5, heads, GROUP), lambda i: (back(i), 0, 0, 0)),
             whole(width // 2, state_n),
             whole(width // 2, state_n),
             whole(width + heads, state_n),

time: 99.2 us -> 98 us (0.988)
  Pallas kernels: 55.1 us -> 53.9 us
    pallas_call x1, Pallas kernels: 30 us -> 28.6 us  [second_pass(): pl.pallas_call(functools.partial(second_kernel, heads, width // heads), g...]
  transfers between devices with their start and end apart: 5 -> 5, of which waited for: 3 -> 3; matrix products, arithmetic and copies ran while one was open for 1% -> 1% of each run, Pallas kernels for 50% -> 49%
where the time goes in v5:
time: 98 us; the launch traced here: 96.9 us
  Pallas kernels  53.9 us (55%)
  starting transfers between devices  32 us (33%)
  waiting for transfers between devices  6.21 us (6%)
  local copies, waits for them, and re-layouts  3.29 us (3%)
    pallas_call x1, Pallas kernels, second_pass(): pl.pallas_call(functools.partial(second_kernel, heads, width // heads), g...  28.6 us
    pallas_call x1, Pallas kernels, first_pass(): pl.pallas_call(functools.partial(first_kernel, heads, width // heads), gr...  11.6 us
    all_to_all x1, starting transfers between devices, shards(): lax.all_to_all(old_states[0].reshape(streams, -1), 'stream', 0, 0, tiled=...  11.5 us
    all_to_all x1, starting transfers between devices, shards(): lax.all_to_all(dealt.at[old_owner].get(mode='promise_in_bounds'), 'stream...  10.3 us
    all_to_all x1, starting transfers between devices, shards(): gathered = lax.all_to_all(everyone, ('stream', 'seq'), 0, 0, tiled=True)  9.98 us
    pallas_call x1, Pallas kernels, fourth_pass(): pl.pallas_call(functools.partial(fourth_kernel, heads, width // heads), g...  7.39 us
    pallas_call x1, Pallas kernels, third_pass(): pl.pallas_call(functools.partial(third_kernel, heads, width // heads), gr...  6.33 us
    ppermute x1, waiting for transfers between devices, shards(): received = lax.ppermute(sent, 'seq', swap)  2.6 us
  transfers between devices with their start and end apart: 5, of which 3 were waited for; matrix products, arithmetic and copies ran while one was open for 1% of the time, Pallas kernels for 49%

profile of v5, /device:TPU:0, one launch (start us, length us, event | category | flops | bytes accessed | tf_op | source)
XLA Modules:
  0.0 96.9 jit_solution(11837425041835057434)
XLA Ops:
  0.6 11.5 %all-to-all-start = ((f32[64,1,1536]{2,1,0:T(1,128)}), f32[64,1,1536]{2,1,0:T(1,128)S(1)}, u32[]{:S(2)}, u32[]{:S(2)}) async-start(f32[64,1,1536]{2,1,0:T(1,128)} %bitcast.34), calls=%async_computation | async-start | bytes 786432 | tf_op jit(solution)/shard_map/all_to_all | solution.py:705
  12.2 0.6 add_bitcast_fusion.base_ref
  12.7 0.0 copy-start.2
  12.7 11.6 %first_pass.1 = (bf16[6,1536,128]{2,1,0:T(8,128)(2,1)}, bf16[6,1536,128]{2,1,0:T(8,128)(2,1)}, f32[6,24,128]{2,1,0:T(8,128)}, f32[1560,128]{1,0:T(8,128)}, f32[7...) custom-call(s32[1,2]{1,0:T(1,128)} %doc_ref.3, s32[1,2]{1,0:T(1,128)} %add_bitcast_fusion.base_ref, bf16[1536,1536]{1,0:T(8,128)(2,1)} %bitcast.28, ...), custom_call_target="tpu_custom_call" | custom-call | flops 1207959552 | bytes 28311552 | tf_op jit(solution)/shard_map/first_pass/pallas_call | solution.py:177
  24.3 0.0 all-to-all-done
  24.4 0.1 collective-permute-start
  24.5 0.0 copy-done.2
  24.5 2.6 %collective-permute-done.exit_ref.received_ref = f32[1560,128]{1,0:T(8,128)} collective-permute-done((f32[1560,128]{1,0:T(8,128)}, f32[1560,128]{1,0:T(8,128)}, u32[]{:S(2)}, u32[]{:S(2)}) %collective-permute-start) | collective-permute-done | bytes 798752 | tf_op jit(solution)/shard_map/ppermute | solution.py:710
  27.1 0.7 gather_fusion
  27.8 1.2 %copy.17 = f32[64,1,1536]{2,1,0:T(1,128)} copy(f32[64,1,1536]{2,0,1:T(8,128)S(1)} %bitcast.33) | data formatting | bytes 786432 | tf_op jit(solution)/shard_map/all_to_all | solution.py:712
  29.0 10.3 %all-to-all-start.1 = ((f32[64,1,1536]{2,1,0:T(1,128)}), f32[64,1,1536]{2,1,0:T(1,128)S(1)}, u32[]{:S(2)}, u32[]{:S(2)}) async-start(f32[64,1,1536]{2,1,0:T(1,128)} %copy.17), calls=%async_computation.1 | async-start | bytes 786432 | tf_op jit(solution)/shard_map/all_to_all | solution.py:712
  39.3 28.6 %second_pass.1 = (bf16[6,1536,256]{2,1,0:T(8,128)(2,1)}, bf16[1536,1536]{1,0:T(8,128)(2,1)}, f32[6,256,256]{2,1,0:T(8,128)}, f32[6,24,256]{2,1,0:T(8,128)}, f32[...) custom-call(s32[1,2]{1,0:T(1,128)} %doc_ref.3, s32[1,2]{1,0:T(1,128)} %add_bitcast_fusion.base_ref, ...), custom_call_target="tpu_custom_call" | custom-call | flops 6039797760 | bytes 33030144 | tf_op jit(solution)/shard_map/second_pass/pallas_call | solution.py:421
  67.9 0.0 all-to-all-done.1
  68.0 0.0 copy-start
  68.0 0.1 collective-permute-start.1
  68.1 1.7 %collective-permute-done.1.other_ref = f32[768,128]{1,0:T(8,128)S(1)} collective-permute-done((f32[768,128]{1,0:T(8,128)S(1)}, f32[768,128]{1,0:T(8,128)S(1)}, u32[]{:S(2)}, u32[]{:S(2)}) %collective-permute-start.1) | collective-permute-done | bytes 393248 | tf_op jit(solution)/shard_map/ppermute | solution.py:720
  69.8 0.0 copy-start.1
  69.8 0.0 copy-done
  69.8 0.7 copy-done.1
  70.6 6.3 %third_pass.1 = (f32[24,1536]{1,0:T(8,128)}, f32[128,128]{1,0:T(8,128)}, bf16[1536,128]{1,0:T(8,128)(2,1)}) custom-call(s32[1,2]{1,0:T(1,128)} %add_bitcast_fusion.base_ref, bf16[6,1536,256]{2,1,0:T(8,128)(2,1)} %get-tuple-element.41.dyt_ref, bf16[1536,256]{1,0:T(8,128)(2,1)} %bitcast.26, f32[6,24,256]{2,1,0:T(8,128)} %get-tuple-element.44.dlogits_in, ...), custom_call_target="tpu_custom_call" | custom-call | flops 603979776 | bytes 4718592 | tf_op jit(solution)/shard_map/third_pass/pallas_call | solution.py:574
  76.9 10.0 %all-to-all-start.2 = ((f32[128,1,128]{2,1,0:T(1,128)}), f32[128,1,128]{2,1,0:T(1,128)S(1)}, u32[]{:S(2)}, u32[]{:S(2)}) async-start(f32[128,1,128]{2,1,0:T(1,128)} %bitcast.36), calls=%async_computation.2 | async-start | bytes 131072 | tf_op jit(solution)/shard_map/all_to_all | solution.py:725
  86.9 7.4 %fourth_pass.1 = (bf16[1536,1536]{1,0:T(8,128)(2,1)}, bf16[1536,256]{1,0:T(8,128)(2,1)}) custom-call(bf16[6,1536,256]{2,1,0:T(8,128)(2,1)} %get-tuple-element.40.yt_ref, bf16[6,1536,256]{2,1,0:T(8,128)(2,1)} %get-tuple-element.41.dyt_ref, bf16[1536,256]{1,0:T(8,128)(2,1)} %bitcast.27, f32[6,256,256]{2,1,0:T(8,128)} %get-tuple-element.42.dmaps_in, ...), custom_call_target="tpu_custom_call" | custom-call | flops 1207959552 | bytes 14155776 | tf_op jit(solution)/shard_map/fourth_pass/pallas_call | solution.py:651
  94.3 1.9 %all-to-all-done.2 = f32[128,1,128]{2,1,0:T(1,128)S(1)} async-done(((f32[128,1,128]{2,1,0:T(1,128)}), f32[128,1,128]{2,1,0:T(1,128)S(1)}, u32[]{:S(2)}, u32[]{:S(2)}) %all-to-all-start.2) | async-done | bytes 65568 | tf_op jit(solution)/shard_map/all_to_all | solution.py:725
  96.2 0.2 reduce_sum.9
  96.3 0.6 fusion
  (5 shorter events, 0.1 us)
Async XLA Ops:
  0.6 23.7 %all-to-all-start = ((f32[64,1,1536]{2,1,0:T(1,128)}), f32[64,1,1536]{2,1,0:T(1,128)S(1)}, u32[]{:S(2)}, u32[]{:S(2)}) async-start(f32[64,1,1536]{2,1,0:T(1,128)} %bitcast.34), calls=%async_computation | async-start | bytes 786432 | tf_op jit(solution)/shard_map/all_to_all | solution.py:705
  12.7 11.7 %copy-start.2 = (s32[64]{0:T(128)S(1)}, s32[64]{0:T(128)}, u32[]{:S(2)}) copy-start(s32[64]{0:T(128)} %param.17) | copy-start | bytes 772
  24.4 2.7 %collective-permute-start = (f32[1560,128]{1,0:T(8,128)}, f32[1560,128]{1,0:T(8,128)}, u32[]{:S(2)}, u32[]{:S(2)}) collective-permute-start(f32[1560,128]{1,0:T(8,128)} %get-tuple-element.38.total_ref), channel_id=1, source_target_pairs={{0,1},{1,0},{2,3},{3,2},{4,5},{5,4},{6,7},{7,6},{8,9},{9,8},{10,11... | collective-permute-start | bytes 2396168 | tf_op jit(solution)/shard_map/ppermute | solution.py:710
  29.0 38.9 %all-to-all-start.1 = ((f32[64,1,1536]{2,1,0:T(1,128)}), f32[64,1,1536]{2,1,0:T(1,128)S(1)}, u32[]{:S(2)}, u32[]{:S(2)}) async-start(f32[64,1,1536]{2,1,0:T(1,128)} %copy.17), calls=%async_computation.1 | async-start | bytes 786432 | tf_op jit(solution)/shard_map/all_to_all | solution.py:712
  68.0 1.8 %copy-start = (f32[768,128]{1,0:T(8,128)}, f32[768,128]{1,0:T(8,128)S(1)}, u32[]{:S(2)}) copy-start(f32[768,128]{1,0:T(8,128)S(1)} %reshape.28.own_ref) | copy-start | bytes 1179652
  68.0 1.8 %collective-permute-start.1 = (f32[768,128]{1,0:T(8,128)S(1)}, f32[768,128]{1,0:T(8,128)S(1)}, u32[]{:S(2)}, u32[]{:S(2)}) collective-permute-start(f32[768,128]{1,0:T(8,128)S(1)} %reshape.28.own_ref), channel_id=1, source_target_pairs={{0,1},{1,0},{2,3},{3,2},{4,5},{5,4},{6,7},{7,6},{8,9},{9,8},{10,11... | collective-permute-start | bytes 1179656 | tf_op jit(solution)/shard_map/ppermute | solution.py:720
  69.8 0.7 copy-start.1
  76.9 19.3 %all-to-all-start.2 = ((f32[128,1,128]{2,1,0:T(1,128)}), f32[128,1,128]{2,1,0:T(1,128)S(1)}, u32[]{:S(2)}, u32[]{:S(2)}) async-start(f32[128,1,128]{2,1,0:T(1,128)} %bitcast.36), calls=%async_computation.2 | async-start | bytes 131072 | tf_op jit(solution)/shard_map/all_to_all | solution.py:725
